TPU v7x, 128 devices: a whole 4x4x4 slice. The times are simulated.
128 devices in a mesh: segment: 4 (over x_lo, core), expert: 32 (over x_hi, z, y).
Axes of the slice: x: 4 (x_hi: 2, x_lo: 2; x = x_hi * 2 + x_lo), y: 4, z: 4, core: 2. Of those that a mesh axis runs over, the one named last changes fastest.
Arguments:
- inputs: bfloat16 [2, 2048, 2560], P(None, 'expert'), may hold values from -6 to 6
- cotangent: bfloat16 [2, 2048, 2560], P(None, 'expert'), may hold values from -6 to 6
- norm_gain: float32 [4, 2560], P('segment'), may hold values from 0.5 to 1.5
- routes: int32 [4, 2, 2048, 6], P('segment', None, 'expert'), may hold values from 0 to 31, all different within a row; in each aligned block of 64 rows (0 to 63, 64 to 127, ..., all dimensions but the last counted through in order) at most 16 rows name the same one
- route_gates: float32 [4, 2, 2048, 6], P('segment', None, 'expert'), may hold values from 0.05 to 1
- w_gate: bfloat16 [4, 32, 2560, 768], P('segment', 'expert'), may hold values from -0.125 to 0.125
- w_up: bfloat16 [4, 32, 2560, 768], P('segment', 'expert'), may hold values from -0.125 to 0.125
- w_down: bfloat16 [4, 32, 768, 2560], P('segment', 'expert'), may hold values from -0.21875 to 0.21875
Outputs:
- states: bfloat16 [4, 2, 2048, 2560], P('segment', None, 'expert')
- input_grads: bfloat16 [4, 2, 2048, 2560], P('segment', None, 'expert')
Inputs may be any that keep to these rules, and one draw needn't show every extreme that they name: `routes`: within the 64 tokens of one device in one micro-batch and layer, no expert is named by more than 16 tokens, a bound that some block reaches; each token names 6 different experts.
All inputs are finite; a program needn't handle non-finite values.
Results may differ from a plain program's by a relative error of at most 0.024.
Values may be sent and summed in bfloat16 or wider, within the bound.
No kernel may reach another device: no remote copies, remote signals or barrier semaphores. Data moves between devices by JAX's collectives and lax.ppermute only.
A program may use at most 192 MiB of HBM per device.

v0:
```python
import jax
import jax.numpy as jnp
from jax import lax
from jax.sharding import PartitionSpec as P

TOP = 6


epsilon = 1e-06


def passed_along(shard, axis, by):
    peers = lax.axis_size(axis)
    pairs = [(i, i + by) for i in range(peers) if 0 <= i + by < peers]
    return lax.ppermute(shard, axis, pairs)


def slot_table(route_block, experts, capacity):
    flat_ids = route_block.reshape(-1)
    onehot = (flat_ids[:, None] == jnp.arange(experts, dtype=jnp.int32)[None, :]).astype(jnp.int32)
    before = jnp.cumsum(onehot, axis=0) - onehot
    position = jnp.sum(before * onehot, axis=1)
    return (flat_ids * capacity + position).reshape(route_block.shape)


def expert_forward(row_block, gate_mat, up_mat, down_mat):
    gate_pre = jnp.dot(row_block, gate_mat, preferred_element_type=jnp.float32)
    up_val = jnp.dot(row_block, up_mat, preferred_element_type=jnp.float32)
    activated = (jax.nn.silu(gate_pre) * up_val).astype(jnp.bfloat16)
    expert_out = jnp.dot(activated, down_mat, preferred_element_type=jnp.float32).astype(
        jnp.bfloat16
    )
    return (expert_out, gate_pre, up_val)


def expert_backward(d_out, gate_pre, up_val, gate_mat, up_mat, down_mat):
    contract = (((1,), (1,)), ((), ()))
    d_act = lax.dot_general(d_out, down_mat, contract, preferred_element_type=jnp.float32)
    sigmoid_g = jax.nn.sigmoid(gate_pre)
    d_gate = (d_act * up_val * sigmoid_g * (1.0 + gate_pre * (1.0 - sigmoid_g))).astype(
        jnp.bfloat16
    )
    d_up = (d_act * gate_pre * sigmoid_g).astype(jnp.bfloat16)
    summed = lax.dot_general(d_gate, gate_mat, contract, preferred_element_type=jnp.float32)
    summed = summed + lax.dot_general(d_up, up_mat, contract, preferred_element_type=jnp.float32)
    return summed.astype(jnp.bfloat16)


def guarded_forward(active, row_block, gate_mat, up_mat, down_mat):

    def run_expert(block_rows):
        return expert_forward(block_rows, gate_mat, up_mat, down_mat)

    def skip_expert(block_rows):
        zero_hidden = jnp.zeros((block_rows.shape[0], gate_mat.shape[1]), jnp.float32)
        return (jnp.zeros(block_rows.shape, jnp.bfloat16), zero_hidden, zero_hidden)

    return lax.cond(active, run_expert, skip_expert, row_block)


def guarded_backward(active, row_block, gate_pre, up_val, gate_mat, up_mat, down_mat):

    def run_expert(pieces):
        return expert_backward(pieces[0], pieces[1], pieces[2], gate_mat, up_mat, down_mat)

    def skip_expert(pieces):
        return jnp.zeros(pieces[0].shape, jnp.bfloat16)

    return lax.cond(active, run_expert, skip_expert, (row_block, gate_pre, up_val))


def store_row(buffer, new_row, chosen, active):
    previous = lax.dynamic_index_in_dim(buffer, chosen, 0, keepdims=False)
    updated = jnp.where(active, new_row, previous)
    return lax.dynamic_update_index_in_dim(buffer, updated, chosen, 0)


def forward_layer(
    layer_in, route_now, gate_now, gain_row, gate_mat, up_mat, down_mat, active, experts, capacity
):
    tok_rows, feat_width = layer_in.shape
    top_count = route_now.shape[1]
    wide_in = layer_in.astype(jnp.float32)
    inv_rms = lax.rsqrt(jnp.mean(wide_in * wide_in, axis=1, keepdims=True) + epsilon)
    normed = (wide_in * inv_rms * gain_row).astype(jnp.bfloat16)
    slot_ids = slot_table(route_now, experts, capacity)
    spread = jnp.broadcast_to(normed[:, None, :], (tok_rows, top_count, feat_width)).reshape(
        -1, feat_width
    )
    outbound = (
        jnp.zeros((experts * capacity, feat_width), jnp.bfloat16)
        .at[slot_ids.reshape(-1)]
        .set(spread)
    )
    outbound = outbound.reshape(experts, capacity, feat_width)
    arrived = lax.all_to_all(outbound, "expert", split_axis=0, concat_axis=0, tiled=True)
    result, gate_pre, up_val = guarded_forward(
        active, arrived.reshape(-1, feat_width), gate_mat, up_mat, down_mat
    )
    returned = lax.all_to_all(
        result.reshape(arrived.shape), "expert", split_axis=0, concat_axis=0, tiled=True
    )
    picked = returned.reshape(-1, feat_width)[slot_ids]
    mixed_sum = jnp.sum(gate_now[:, :, None] * picked.astype(jnp.float32), axis=1)
    return ((wide_in + mixed_sum).astype(jnp.bfloat16), gate_pre, up_val)


def backward_layer(
    d_in,
    layer_in,
    route_now,
    gate_now,
    gain_row,
    gate_pre,
    up_val,
    gate_mat,
    up_mat,
    down_mat,
    active,
    experts,
    capacity,
):
    feat_width = layer_in.shape[1]
    wide_in = layer_in.astype(jnp.float32)
    inv_rms = lax.rsqrt(jnp.mean(wide_in * wide_in, axis=1, keepdims=True) + epsilon)
    d_wide = d_in.astype(jnp.float32)
    slot_ids = slot_table(route_now, experts, capacity)
    d_out = (gate_now[:, :, None] * d_wide[:, None, :]).astype(jnp.bfloat16).reshape(-1, feat_width)
    outbound = (
        jnp.zeros((experts * capacity, feat_width), jnp.bfloat16)
        .at[slot_ids.reshape(-1)]
        .set(d_out)
    )
    outbound = outbound.reshape(experts, capacity, feat_width)
    arrived = lax.all_to_all(outbound, "expert", split_axis=0, concat_axis=0, tiled=True)
    d_rows = guarded_backward(
        active, arrived.reshape(-1, feat_width), gate_pre, up_val, gate_mat, up_mat, down_mat
    )
    returned = lax.all_to_all(
        d_rows.reshape(arrived.shape), "expert", split_axis=0, concat_axis=0, tiled=True
    )
    d_norm = jnp.sum(returned.reshape(-1, feat_width)[slot_ids].astype(jnp.float32), axis=1)
    scaled = gain_row * d_norm
    inner = jnp.mean(wide_in * scaled, axis=1, keepdims=True)
    cubed = inv_rms * inv_rms * inv_rms
    return (d_wide + inv_rms * scaled - wide_in * cubed * inner).astype(jnp.bfloat16)


def local(inputs, cotangent, norm_gain, routes, route_gates, w_gate, w_up, w_down):
    segment_id = lax.axis_index("segment")
    segments = lax.axis_size("segment")
    sources = lax.axis_size("expert")
    micro_count, tok_rows, feat_width = inputs.shape
    experts = sources * w_gate.shape[1]
    capacity = min(tok_rows, 4 * tok_rows * TOP // (3 * experts))
    hidden = w_gate.shape[3]
    gate_mat = w_gate[0, 0]
    up_mat = w_up[0, 0]
    down_mat = w_down[0, 0]
    gain_row = norm_gain[0]
    route_all = routes[0]
    gate_all = route_gates[0]
    tick_count = micro_count + segments - 1
    saved_in = jnp.zeros((micro_count, tok_rows, feat_width), jnp.bfloat16)
    states = jnp.zeros((micro_count, tok_rows, feat_width), jnp.bfloat16)
    kept_gate = jnp.zeros((micro_count, experts * capacity, hidden), jnp.float32)
    kept_up = jnp.zeros((micro_count, experts * capacity, hidden), jnp.float32)
    incoming = jnp.zeros((tok_rows, feat_width), jnp.bfloat16)
    for tick_no in range(tick_count):
        micro_at = tick_no - segment_id
        active = (micro_at >= 0) & (micro_at < micro_count)
        chosen = jnp.clip(micro_at, 0, micro_count - 1)
        first_in = lax.dynamic_index_in_dim(inputs, chosen, 0, keepdims=False)
        layer_in = jnp.where(segment_id == 0, first_in, incoming)
        route_now = lax.dynamic_index_in_dim(route_all, chosen, 0, keepdims=False)
        gate_now = lax.dynamic_index_in_dim(gate_all, chosen, 0, keepdims=False)
        layer_out, gate_pre, up_val = forward_layer(
            layer_in,
            route_now,
            gate_now,
            gain_row,
            gate_mat,
            up_mat,
            down_mat,
            active,
            experts,
            capacity,
        )
        saved_in = store_row(saved_in, layer_in, chosen, active)
        states = store_row(states, layer_out, chosen, active)
        kept_gate = store_row(kept_gate, gate_pre, chosen, active)
        kept_up = store_row(kept_up, up_val, chosen, active)
        if tick_no + 1 < tick_count:
            incoming = passed_along(layer_out, "segment", 1)
    input_grads = jnp.zeros((micro_count, tok_rows, feat_width), jnp.bfloat16)
    incoming = jnp.zeros((tok_rows, feat_width), jnp.bfloat16)
    for tick_no in range(tick_count):
        micro_at = tick_no - (segments - 1 - segment_id)
        active = (micro_at >= 0) & (micro_at < micro_count)
        chosen = jnp.clip(micro_at, 0, micro_count - 1)
        last_in = lax.dynamic_index_in_dim(cotangent, chosen, 0, keepdims=False)
        d_in = jnp.where(segment_id == segments - 1, last_in, incoming)
        layer_in = lax.dynamic_index_in_dim(saved_in, chosen, 0, keepdims=False)
        route_now = lax.dynamic_index_in_dim(route_all, chosen, 0, keepdims=False)
        gate_now = lax.dynamic_index_in_dim(gate_all, chosen, 0, keepdims=False)
        gate_pre = lax.dynamic_index_in_dim(kept_gate, chosen, 0, keepdims=False)
        up_val = lax.dynamic_index_in_dim(kept_up, chosen, 0, keepdims=False)
        d_prev = backward_layer(
            d_in,
            layer_in,
            route_now,
            gate_now,
            gain_row,
            gate_pre,
            up_val,
            gate_mat,
            up_mat,
            down_mat,
            active,
            experts,
            capacity,
        )
        input_grads = store_row(input_grads, d_prev, chosen, active)
        if tick_no + 1 < tick_count:
            incoming = passed_along(d_prev, "segment", -1)
    return (states[None], input_grads[None])


def solution(mesh):
    placed = (
        P(None, "expert", None),
        P(None, "expert", None),
        P("segment", None),
        P("segment", None, "expert", None),
        P("segment", None, "expert", None),
        P("segment", "expert", None, None),
        P("segment", "expert", None, None),
        P("segment", "expert", None, None),
    )
    return jax.shard_map(
        local,
        mesh=mesh,
        in_specs=placed,
        out_specs=(P("segment", None, "expert", None), P("segment", None, "expert", None)),
        check_vma=False,
    )
```

profile of v0, /device:TPU:1, one launch (start us, length us, event | category | flops | bytes accessed | tf_op | source)
XLA Modules:
  0.0 1158.7 jit_solution(15059816744654920454)
XLA Ops:
  17.6 11.3 all-to-all-start
  28.9 32.3 %all-to-all-done = bf16[32,16,2560]{2,1,0:T(8,128)(2,1)S(1)} async-done(((bf16[32,16,2560]{2,1,0:T(8,128)(2,1)}), bf16[32,16,2560]{2,1,0:T(8,128)(2,1)S(1)}, u32[]{:S(2)}, u32[]{:S(2)}) %all-to-all-start) | async-done | bytes 2621472 | tf_op jit(solution)/shard_map/all_to_all | solution.py:96
  65.5 8.9 all-to-all-start.1
  76.5 21.8 %all-to-all-done.1 = bf16[32,16,2560]{2,1,0:T(8,128)(2,1)S(1)} async-done(((bf16[32,16,2560]{2,1,0:T(8,128)(2,1)}), bf16[32,16,2560]{2,1,0:T(8,128)(2,1)S(1)}, u32[]{:S(2)}, u32[]{:S(2)}) %all-to-all-start.1) | async-done | bytes 2621472 | tf_op jit(solution)/shard_map/all_to_all | solution.py:100
  110.7 13.4 %collective-permute-start = (bf16[64,2560]{1,0:T(8,128)(2,1)S(1)}, bf16[64,2560]{1,0:T(8,128)(2,1)S(1)}, u32[]{:S(2)}, u32[]{:S(2)}) collective-permute-start(bf16[64,2560]{1,0:T(8,128)(2,1)S(1)} %fusion.134), channel_id=1, source_target_pairs={{0,32},{32,64},{64,96},{1,33},{33,65},{65,97},{2,34},{34,66},{66,9... | collective-permute-start | bytes 983048 | tf_op jit(solution)/shard_map/ppermute | solution.py:15
  138.1 6.8 all-to-all-start.2
  145.0 31.9 %all-to-all-done.2 = bf16[32,16,2560]{2,1,0:T(8,128)(2,1)S(1)} async-done(((bf16[32,16,2560]{2,1,0:T(8,128)(2,1)}), bf16[32,16,2560]{2,1,0:T(8,128)(2,1)S(1)}, u32[]{:S(2)}, u32[]{:S(2)}) %all-to-all-start.2) | async-done | bytes 2621472 | tf_op jit(solution)/shard_map/all_to_all | solution.py:96
  176.8 13.5 %conditional.11 = (bf16[512,2560]{1,0:T(8,128)(2,1)S(1)}, f32[512,768]{1,0:T(8,128)}, f32[512,768]{1,0:T(8,128)}) conditional(s32[]{:T(128)} %convert_element_type.404, () %tuple.100, (bf16[32,16,2560]{2,1,0:T(8,128)(2,1)S(1)}, bf16[2560,768]{1,0:T(8,128)(2,1)}, bf16[2560,768]{1,0:T(8,128)(2,1)}, bf16[768,2560]{1,0:T(8,128)(2,1)}) %tuple.204), branch_computations={%region_13.14_spmd, %region_14.15_spmd} | conditional | flops 6043467776 | bytes 57409616 | solution.py:58
  191.9 7.2 all-to-all-start.3
  211.0 24.0 %all-to-all-done.3 = bf16[32,16,2560]{2,1,0:T(8,128)(2,1)S(1)} async-done(((bf16[32,16,2560]{2,1,0:T(8,128)(2,1)}), bf16[32,16,2560]{2,1,0:T(8,128)(2,1)S(1)}, u32[]{:S(2)}, u32[]{:S(2)}) %all-to-all-start.3) | async-done | bytes 2621472 | tf_op jit(solution)/shard_map/all_to_all | solution.py:100
  263.4 6.6 all-to-all-start.4
  270.0 33.1 %all-to-all-done.4 = bf16[32,16,2560]{2,1,0:T(8,128)(2,1)S(1)} async-done(((bf16[32,16,2560]{2,1,0:T(8,128)(2,1)}), bf16[32,16,2560]{2,1,0:T(8,128)(2,1)S(1)}, u32[]{:S(2)}, u32[]{:S(2)}) %all-to-all-start.4) | async-done | bytes 2621472 | tf_op jit(solution)/shard_map/all_to_all | solution.py:96
  303.2 13.1 %conditional.12 = (bf16[512,2560]{1,0:T(8,128)(2,1)S(1)}, f32[512,768]{1,0:T(8,128)}, f32[512,768]{1,0:T(8,128)}) conditional(s32[]{:T(128)} %convert_element_type.411, () %tuple.102, (bf16[32,16,2560]{2,1,0:T(8,128)(2,1)S(1)}, bf16[2560,768]{1,0:T(8,128)(2,1)}, bf16[2560,768]{1,0:T(8,128)(2,1)}, bf16[768,2560]{1,0:T(8,128)(2,1)}) %tuple.205), branch_computations={%region_21.22_spmd, %region_22.23_spmd} | conditional | flops 6043467776 | bytes 57409616 | solution.py:58
  317.9 6.8 all-to-all-start.5
  326.9 24.2 %all-to-all-done.5 = bf16[32,16,2560]{2,1,0:T(8,128)(2,1)S(1)} async-done(((bf16[32,16,2560]{2,1,0:T(8,128)(2,1)}), bf16[32,16,2560]{2,1,0:T(8,128)(2,1)S(1)}, u32[]{:S(2)}, u32[]{:S(2)}) %all-to-all-start.5) | async-done | bytes 2621472 | tf_op jit(solution)/shard_map/all_to_all | solution.py:100
  373.0 6.2 scatter_custom_fusion.3
  384.7 33.1 %all-to-all-done.6 = bf16[32,16,2560]{2,1,0:T(8,128)(2,1)S(1)} async-done(((bf16[32,16,2560]{2,1,0:T(8,128)(2,1)}), bf16[32,16,2560]{2,1,0:T(8,128)(2,1)S(1)}, u32[]{:S(2)}, u32[]{:S(2)}) %all-to-all-start.6) | async-done | bytes 2621472 | tf_op jit(solution)/shard_map/all_to_all | solution.py:96
  422.4 6.6 all-to-all-start.7
  436.0 25.4 %all-to-all-done.7 = bf16[32,16,2560]{2,1,0:T(8,128)(2,1)S(1)} async-done(((bf16[32,16,2560]{2,1,0:T(8,128)(2,1)}), bf16[32,16,2560]{2,1,0:T(8,128)(2,1)S(1)}, u32[]{:S(2)}, u32[]{:S(2)}) %all-to-all-start.7) | async-done | bytes 2621472 | tf_op jit(solution)/shard_map/all_to_all | solution.py:100
  474.0 8.9 collective-permute-start.3
  509.9 6.7 scatter_custom_fusion.5
  531.6 7.9 all-to-all-start.10
  564.1 11.3 all-to-all-done.10
  577.1 7.5 all-to-all-start.11
  589.8 26.9 %all-to-all-done.11 = bf16[32,16,2560]{2,1,0:T(8,128)(2,1)S(1)} async-done(((bf16[32,16,2560]{2,1,0:T(8,128)(2,1)}), bf16[32,16,2560]{2,1,0:T(8,128)(2,1)S(1)}, u32[]{:S(2)}, u32[]{:S(2)}) %all-to-all-start.11) | async-done | bytes 2621472 | tf_op jit(solution)/shard_map/all_to_all | solution.py:139
  647.3 6.8 scatter_custom_fusion.6
  654.1 9.1 all-to-all-start.12
  663.2 32.2 %all-to-all-done.12 = bf16[32,16,2560]{2,1,0:T(8,128)(2,1)S(1)} async-done(((bf16[32,16,2560]{2,1,0:T(8,128)(2,1)}), bf16[32,16,2560]{2,1,0:T(8,128)(2,1)S(1)}, u32[]{:S(2)}, u32[]{:S(2)}) %all-to-all-start.12) | async-done | bytes 2621472 | tf_op jit(solution)/shard_map/all_to_all | solution.py:135
  697.3 7.0 all-to-all-start.13
  707.8 32.1 %all-to-all-done.13 = bf16[32,16,2560]{2,1,0:T(8,128)(2,1)S(1)} async-done(((bf16[32,16,2560]{2,1,0:T(8,128)(2,1)}), bf16[32,16,2560]{2,1,0:T(8,128)(2,1)S(1)}, u32[]{:S(2)}, u32[]{:S(2)}) %all-to-all-start.13) | async-done | bytes 2621472 | tf_op jit(solution)/shard_map/all_to_all | solution.py:139
  758.0 7.8 collective-permute-done.5
  774.7 6.8 scatter_custom_fusion.7
  787.5 29.1 %all-to-all-done.14 = bf16[32,16,2560]{2,1,0:T(8,128)(2,1)S(1)} async-done(((bf16[32,16,2560]{2,1,0:T(8,128)(2,1)}), bf16[32,16,2560]{2,1,0:T(8,128)(2,1)S(1)}, u32[]{:S(2)}, u32[]{:S(2)}) %all-to-all-start.14) | async-done | bytes 2621472 | tf_op jit(solution)/shard_map/all_to_all | solution.py:135
  816.6 11.0 conditional.17
  829.1 7.0 all-to-all-start.15
  843.7 14.6 %all-to-all-done.15 = bf16[32,16,2560]{2,1,0:T(8,128)(2,1)S(1)} async-done(((bf16[32,16,2560]{2,1,0:T(8,128)(2,1)}), bf16[32,16,2560]{2,1,0:T(8,128)(2,1)S(1)}, u32[]{:S(2)}, u32[]{:S(2)}) %all-to-all-start.15) | async-done | bytes 2621472 | tf_op jit(solution)/shard_map/all_to_all | solution.py:139
  873.0 9.5 collective-permute-done.6
  891.5 6.8 scatter_custom_fusion.8
  902.7 28.4 %all-to-all-done.16 = bf16[32,16,2560]{2,1,0:T(8,128)(2,1)S(1)} async-done(((bf16[32,16,2560]{2,1,0:T(8,128)(2,1)}), bf16[32,16,2560]{2,1,0:T(8,128)(2,1)S(1)}, u32[]{:S(2)}, u32[]{:S(2)}) %all-to-all-start.16) | async-done | bytes 2621472 | tf_op jit(solution)/shard_map/all_to_all | solution.py:135
  931.1 11.2 conditional.18
  943.9 6.3 all-to-all-start.17
  952.2 33.5 %all-to-all-done.17 = bf16[32,16,2560]{2,1,0:T(8,128)(2,1)S(1)} async-done(((bf16[32,16,2560]{2,1,0:T(8,128)(2,1)}), bf16[32,16,2560]{2,1,0:T(8,128)(2,1)S(1)}, u32[]{:S(2)}, u32[]{:S(2)}) %all-to-all-start.17) | async-done | bytes 2621472 | tf_op jit(solution)/shard_map/all_to_all | solution.py:139
  1002.3 6.2 collective-permute-done.7
  1023.3 37.8 %all_to_all.100 = bf16[32,16,2560]{2,1,0:T(8,128)(2,1)} all-to-all(bf16[32,16,2560]{2,1,0:T(8,128)(2,1)S(1)} %bitcast.833), channel_id=1, replica_groups=mesh['segment'=4,'expert'=32] {'expert'}, dimensions={0} | all-to-all | bytes 5242880 | tf_op jit(solution)/shard_map/all_to_all | solution.py:135
  1067.0 34.3 %all-to-all-done.9 = bf16[32,16,2560]{2,1,0:T(8,128)(2,1)S(1)} async-done(((bf16[32,16,2560]{2,1,0:T(8,128)(2,1)}), bf16[32,16,2560]{2,1,0:T(8,128)(2,1)S(1)}, u32[]{:S(2)}, u32[]{:S(2)}) %all-to-all-start.9) | async-done | bytes 2621472 | tf_op jit(solution)/shard_map/all_to_all | solution.py:100
  1101.3 8.5 all-to-all-start.19
  1126.7 15.8 %all-to-all-done.19 = bf16[32,16,2560]{2,1,0:T(8,128)(2,1)} async-done(((bf16[32,16,2560]{2,1,0:T(8,128)(2,1)}), bf16[32,16,2560]{2,1,0:T(8,128)(2,1)}, u32[]{:S(2)}, u32[]{:S(2)}) %all-to-all-start.19) | async-done | bytes 2621472 | tf_op jit(solution)/shard_map/all_to_all | solution.py:139
  1142.5 7.3 gather_fusion.9
  (536 shorter events, 450.9 us)
Async XLA Ops:
  17.6 43.7 %all-to-all-start = ((bf16[32,16,2560]{2,1,0:T(8,128)(2,1)}), bf16[32,16,2560]{2,1,0:T(8,128)(2,1)S(1)}, u32[]{:S(2)}, u32[]{:S(2)}) async-start(bf16[32,16,2560]{2,1,0:T(8,128)(2,1)} %bitcast.23), calls=%async_computation | async-start | bytes 5242880 | tf_op jit(solution)/shard_map/all_to_all | solution.py:96
  65.5 9.2 copy-start.70
  65.5 32.9 %all-to-all-start.1 = ((bf16[32,16,2560]{2,1,0:T(8,128)(2,1)}), bf16[32,16,2560]{2,1,0:T(8,128)(2,1)S(1)}, u32[]{:S(2)}, u32[]{:S(2)}) async-start(bf16[32,16,2560]{2,1,0:T(8,128)(2,1)} %bitcast.834), calls=%async_computation.1 | async-start | bytes 5242880 | tf_op jit(solution)/shard_map/all_to_all | solution.py:100
  110.7 17.4 %collective-permute-start = (bf16[64,2560]{1,0:T(8,128)(2,1)S(1)}, bf16[64,2560]{1,0:T(8,128)(2,1)S(1)}, u32[]{:S(2)}, u32[]{:S(2)}) collective-permute-start(bf16[64,2560]{1,0:T(8,128)(2,1)S(1)} %fusion.134), channel_id=1, source_target_pairs={{0,32},{32,64},{64,96},{1,33},{33,65},{65,97},{2,34},{34,66},{66,9... | collective-permute-start | bytes 983048 | tf_op jit(solution)/shard_map/ppermute | solution.py:15
  138.1 38.7 %all-to-all-start.2 = ((bf16[32,16,2560]{2,1,0:T(8,128)(2,1)}), bf16[32,16,2560]{2,1,0:T(8,128)(2,1)S(1)}, u32[]{:S(2)}, u32[]{:S(2)}) async-start(bf16[32,16,2560]{2,1,0:T(8,128)(2,1)} %bitcast.34), calls=%async_computation.2 | async-start | bytes 5242880 | tf_op jit(solution)/shard_map/all_to_all | solution.py:96
  191.9 43.1 %all-to-all-start.3 = ((bf16[32,16,2560]{2,1,0:T(8,128)(2,1)}), bf16[32,16,2560]{2,1,0:T(8,128)(2,1)S(1)}, u32[]{:S(2)}, u32[]{:S(2)}) async-start(bf16[32,16,2560]{2,1,0:T(8,128)(2,1)} %bitcast.835), calls=%async_computation.3 | async-start | bytes 5242880 | tf_op jit(solution)/shard_map/all_to_all | solution.py:100
  247.7 6.1 collective-permute-start.1
  263.4 39.8 %all-to-all-start.4 = ((bf16[32,16,2560]{2,1,0:T(8,128)(2,1)}), bf16[32,16,2560]{2,1,0:T(8,128)(2,1)S(1)}, u32[]{:S(2)}, u32[]{:S(2)}) async-start(bf16[32,16,2560]{2,1,0:T(8,128)(2,1)} %bitcast.43), calls=%async_computation.4 | async-start | bytes 5242880 | tf_op jit(solution)/shard_map/all_to_all | solution.py:96
  317.9 33.1 %all-to-all-start.5 = ((bf16[32,16,2560]{2,1,0:T(8,128)(2,1)}), bf16[32,16,2560]{2,1,0:T(8,128)(2,1)S(1)}, u32[]{:S(2)}, u32[]{:S(2)}) async-start(bf16[32,16,2560]{2,1,0:T(8,128)(2,1)} %bitcast.836), calls=%async_computation.5 | async-start | bytes 5242880 | tf_op jit(solution)/shard_map/all_to_all | solution.py:100
  363.6 6.1 collective-permute-start.2
  379.3 38.6 %all-to-all-start.6 = ((bf16[32,16,2560]{2,1,0:T(8,128)(2,1)}), bf16[32,16,2560]{2,1,0:T(8,128)(2,1)S(1)}, u32[]{:S(2)}, u32[]{:S(2)}) async-start(bf16[32,16,2560]{2,1,0:T(8,128)(2,1)} %bitcast.52), calls=%async_computation.6 | async-start | bytes 5242880 | tf_op jit(solution)/shard_map/all_to_all | solution.py:96
  422.4 39.0 %all-to-all-start.7 = ((bf16[32,16,2560]{2,1,0:T(8,128)(2,1)}), bf16[32,16,2560]{2,1,0:T(8,128)(2,1)S(1)}, u32[]{:S(2)}, u32[]{:S(2)}) async-start(bf16[32,16,2560]{2,1,0:T(8,128)(2,1)} %bitcast.837), calls=%async_computation.7 | async-start | bytes 5242880 | tf_op jit(solution)/shard_map/all_to_all | solution.py:100
  429.6 35.1 %copy-start.64 = (s32[1,1,64,6]{3,2,1,0:T(8,128)}, s32[1,1,64,6]{3,2,1,0:T(8,128)S(1)}, u32[]{:S(2)}) copy-start(s32[1,1,64,6]{3,2,1,0:T(8,128)S(1)} %copy.64) | copy-start | bytes 4612
  434.2 30.5 %copy-start.72 = (s32[384]{0:T(512)}, s32[384]{0:T(512)S(1)}, u32[]{:S(2)}) copy-start(s32[384]{0:T(512)S(1)} %fusion.212) | copy-start | bytes 4612
  473.8 12.9 %copy-start.11 = (bf16[2,64,2560]{2,1,0:T(8,128)(2,1)S(1)}, bf16[2,64,2560]{2,1,0:T(8,128)(2,1)}, u32[]{:S(2)}) copy-start(bf16[2,64,2560]{2,1,0:T(8,128)(2,1)} %param.28) | copy-start | bytes 1966084
  474.0 13.1 %copy-start.27 = (bf16[2,64,2560]{2,1,0:T(8,128)(2,1)}, bf16[2,64,2560]{2,1,0:T(8,128)(2,1)S(1)}, u32[]{:S(2)}) copy-start(bf16[2,64,2560]{2,1,0:T(8,128)(2,1)S(1)} %get-tuple-element.437) | copy-start | bytes 1966084
  474.0 12.7 %collective-permute-start.3 = (bf16[64,2560]{1,0:T(8,128)(2,1)S(1)}, bf16[64,2560]{1,0:T(8,128)(2,1)S(1)}, u32[]{:S(2)}, u32[]{:S(2)}) collective-permute-start(bf16[64,2560]{1,0:T(8,128)(2,1)S(1)} %get-tuple-element.438), channel_id=1, source_target_pairs={{0,32},{32,64},{64,96},{1,33},{33,65},{65,97},{2,34},{34,66},{66,9... | collective-permute-start | bytes 983048 | tf_op jit(solution)/shard_map/ppermute | solution.py:15
  496.3 35.4 %all-to-all-start.8 = ((bf16[32,16,2560]{2,1,0:T(8,128)(2,1)}), bf16[32,16,2560]{2,1,0:T(8,128)(2,1)}, u32[]{:S(2)}, u32[]{:S(2)}) async-start(bf16[32,16,2560]{2,1,0:T(8,128)(2,1)} %bitcast.62), calls=%async_computation.8 | async-start | bytes 5242880 | tf_op jit(solution)/shard_map/all_to_all | solution.py:96
  531.6 43.8 %all-to-all-start.10 = ((bf16[32,16,2560]{2,1,0:T(8,128)(2,1)}), bf16[32,16,2560]{2,1,0:T(8,128)(2,1)}, u32[]{:S(2)}, u32[]{:S(2)}) async-start(bf16[32,16,2560]{2,1,0:T(8,128)(2,1)} %bitcast.79), calls=%async_computation.10 | async-start | bytes 5242880 | tf_op jit(solution)/shard_map/all_to_all | solution.py:135
  577.1 7.6 copy-start.81
  577.1 8.0 copy-start.80
  577.1 12.4 %copy-start.82 = (f32[1,1,64,6]{2,1,3,0:T(1,128)S(1)}, f32[1,1,64,6]{2,1,3,0:T(1,128)}, u32[]{:S(2)}) copy-start(f32[1,1,64,6]{2,1,3,0:T(1,128)} %get-tuple-element.450) | copy-start | bytes 4612
  577.1 39.6 %all-to-all-start.11 = ((bf16[32,16,2560]{2,1,0:T(8,128)(2,1)}), bf16[32,16,2560]{2,1,0:T(8,128)(2,1)S(1)}, u32[]{:S(2)}, u32[]{:S(2)}) async-start(bf16[32,16,2560]{2,1,0:T(8,128)(2,1)} %bitcast.838), calls=%async_computation.11 | async-start | bytes 5242880 | tf_op jit(solution)/shard_map/all_to_all | solution.py:139
  628.6 9.8 copy-start.12
  630.0 8.4 collective-permute-start.4
  654.1 41.3 %all-to-all-start.12 = ((bf16[32,16,2560]{2,1,0:T(8,128)(2,1)}), bf16[32,16,2560]{2,1,0:T(8,128)(2,1)S(1)}, u32[]{:S(2)}, u32[]{:S(2)}) async-start(bf16[32,16,2560]{2,1,0:T(8,128)(2,1)} %bitcast.105), calls=%async_computation.12 | async-start | bytes 5242880 | tf_op jit(solution)/shard_map/all_to_all | solution.py:135
  697.3 42.6 %all-to-all-start.13 = ((bf16[32,16,2560]{2,1,0:T(8,128)(2,1)}), bf16[32,16,2560]{2,1,0:T(8,128)(2,1)S(1)}, u32[]{:S(2)}, u32[]{:S(2)}) async-start(bf16[32,16,2560]{2,1,0:T(8,128)(2,1)} %bitcast.839), calls=%async_computation.13 | async-start | bytes 5242880 | tf_op jit(solution)/shard_map/all_to_all | solution.py:139
  751.8 14.0 %copy-start.39 = (bf16[2,64,2560]{2,1,0:T(8,128)(2,1)S(1)}, bf16[2,64,2560]{2,1,0:T(8,128)(2,1)}, u32[]{:S(2)}) copy-start(bf16[2,64,2560]{2,1,0:T(8,128)(2,1)} %param.29) | copy-start | bytes 1966084
  754.1 20.6 %copy-start.31 = (bf16[2,64,2560]{2,1,0:T(8,128)(2,1)}, bf16[2,64,2560]{2,1,0:T(8,128)(2,1)S(1)}, u32[]{:S(2)}) copy-start(bf16[2,64,2560]{2,1,0:T(8,128)(2,1)S(1)} %get-tuple-element.427) | copy-start | bytes 1966084
  754.1 11.7 %collective-permute-start.5 = (bf16[64,2560]{1,0:T(8,128)(2,1)}, bf16[64,2560]{1,0:T(8,128)(2,1)S(1)}, u32[]{:S(2)}, u32[]{:S(2)}) collective-permute-start(bf16[64,2560]{1,0:T(8,128)(2,1)} %get-tuple-element.428), channel_id=1, source_target_pairs={{32,0},{64,32},{96,64},{33,1},{65,33},{97,65},{34,2},{66,34},{98,6... | collective-permute-start | bytes 983048 | tf_op jit(solution)/shard_map/ppermute | solution.py:15
  781.5 35.1 %all-to-all-start.14 = ((bf16[32,16,2560]{2,1,0:T(8,128)(2,1)}), bf16[32,16,2560]{2,1,0:T(8,128)(2,1)S(1)}, u32[]{:S(2)}, u32[]{:S(2)}) async-start(bf16[32,16,2560]{2,1,0:T(8,128)(2,1)} %bitcast.115), calls=%async_computation.14 | async-start | bytes 5242880 | tf_op jit(solution)/shard_map/all_to_all | solution.py:135
  829.1 7.1 copy-start.77
  829.1 7.5 copy-start.76
  829.1 11.9 %copy-start.78 = (f32[1,1,64,6]{2,1,3,0:T(1,128)S(1)}, f32[1,1,64,6]{2,1,3,0:T(1,128)}, u32[]{:S(2)}) copy-start(f32[1,1,64,6]{2,1,3,0:T(1,128)} %get-tuple-element.453) | copy-start | bytes 4612
  829.1 29.2 %all-to-all-start.15 = ((bf16[32,16,2560]{2,1,0:T(8,128)(2,1)}), bf16[32,16,2560]{2,1,0:T(8,128)(2,1)S(1)}, u32[]{:S(2)}, u32[]{:S(2)}) async-start(bf16[32,16,2560]{2,1,0:T(8,128)(2,1)} %bitcast.840), calls=%async_computation.15 | async-start | bytes 5242880 | tf_op jit(solution)/shard_map/all_to_all | solution.py:139
  870.3 12.3 %copy-start.40 = (bf16[2,64,2560]{2,1,0:T(8,128)(2,1)S(1)}, bf16[2,64,2560]{2,1,0:T(8,128)(2,1)}, u32[]{:S(2)}) copy-start(bf16[2,64,2560]{2,1,0:T(8,128)(2,1)} %param.29) | copy-start | bytes 1966084
  870.9 20.6 %copy-start.33 = (bf16[2,64,2560]{2,1,0:T(8,128)(2,1)}, bf16[2,64,2560]{2,1,0:T(8,128)(2,1)S(1)}, u32[]{:S(2)}) copy-start(bf16[2,64,2560]{2,1,0:T(8,128)(2,1)S(1)} %get-tuple-element.425) | copy-start | bytes 1966084
  870.9 11.7 %collective-permute-start.6 = (bf16[64,2560]{1,0:T(8,128)(2,1)S(1)}, bf16[64,2560]{1,0:T(8,128)(2,1)S(1)}, u32[]{:S(2)}, u32[]{:S(2)}) collective-permute-start(bf16[64,2560]{1,0:T(8,128)(2,1)S(1)} %get-tuple-element.426), channel_id=1, source_target_pairs={{32,0},{64,32},{96,64},{33,1},{65,33},{97,65},{34,2},{66,34},{98,6... | collective-permute-start | bytes 983048 | tf_op jit(solution)/shard_map/ppermute | solution.py:15
  898.3 32.8 %all-to-all-start.16 = ((bf16[32,16,2560]{2,1,0:T(8,128)(2,1)}), bf16[32,16,2560]{2,1,0:T(8,128)(2,1)S(1)}, u32[]{:S(2)}, u32[]{:S(2)}) async-start(bf16[32,16,2560]{2,1,0:T(8,128)(2,1)} %bitcast.125), calls=%async_computation.16 | async-start | bytes 5242880 | tf_op jit(solution)/shard_map/all_to_all | solution.py:135
  943.9 41.9 %all-to-all-start.17 = ((bf16[32,16,2560]{2,1,0:T(8,128)(2,1)}), bf16[32,16,2560]{2,1,0:T(8,128)(2,1)S(1)}, u32[]{:S(2)}, u32[]{:S(2)}) async-start(bf16[32,16,2560]{2,1,0:T(8,128)(2,1)} %bitcast.841), calls=%async_computation.17 | async-start | bytes 5242880 | tf_op jit(solution)/shard_map/all_to_all | solution.py:139
  997.7 10.9 copy-start.41
  1000.0 17.6 %copy-start.35 = (bf16[2,64,2560]{2,1,0:T(8,128)(2,1)}, bf16[2,64,2560]{2,1,0:T(8,128)(2,1)S(1)}, u32[]{:S(2)}) copy-start(bf16[2,64,2560]{2,1,0:T(8,128)(2,1)S(1)} %get-tuple-element.423) | copy-start | bytes 1966084
  1000.0 8.6 collective-permute-start.7
  1061.1 40.1 %all-to-all-start.9 = ((bf16[32,16,2560]{2,1,0:T(8,128)(2,1)}), bf16[32,16,2560]{2,1,0:T(8,128)(2,1)S(1)}, u32[]{:S(2)}, u32[]{:S(2)}) async-start(bf16[32,16,2560]{2,1,0:T(8,128)(2,1)} %bitcast.63), calls=%async_computation.9 | async-start | bytes 5242880 | tf_op jit(solution)/shard_map/all_to_all | solution.py:100
  1101.2 8.7 copy-start.73
  1101.2 9.0 copy-start.65
  1101.3 9.1 copy-start.74
  1101.3 41.3 %all-to-all-start.19 = ((bf16[32,16,2560]{2,1,0:T(8,128)(2,1)}), bf16[32,16,2560]{2,1,0:T(8,128)(2,1)}, u32[]{:S(2)}, u32[]{:S(2)}) async-start(bf16[32,16,2560]{2,1,0:T(8,128)(2,1)} %bitcast.842), calls=%async_computation.19 | async-start | bytes 5242880 | tf_op jit(solution)/shard_map/all_to_all | solution.py:139
  (72 other events, 264.2 us)
where the time goes:
time: 1180 us; the launch traced here: 1160 us
  waiting for transfers between devices  528 us (45%)
  local copies, waits for them, and re-layouts  244 us (21%)
  starting transfers between devices  172 us (15%)
  other arithmetic  125 us (11%)
  matrix products  48.1 us (4%)
  blocking collectives  37.8 us (3%)
    all_to_all x5, waiting for transfers between devices, forward_layer(): lax.all_to_all(outbound, 'expert', split_axis=0, concat_axis=0, tiled=True)  132 us
    all_to_all x5, waiting for transfers between devices, forward_layer(): lax.all_to_all(result.reshape(arrived.shape), 'expert', split_axis=0, con...  130 us
    all_to_all x5, waiting for transfers between devices, backward_layer(): lax.all_to_all(d_rows.reshape(arrived.shape), 'expert', split_axis=0, con...  123 us
    all_to_all x4, waiting for transfers between devices, backward_layer(): lax.all_to_all(outbound, 'expert', split_axis=0, concat_axis=0, tiled=True)  101 us
    ppermute x8, waiting for transfers between devices, passed_along(): return lax.ppermute(shard, axis, pairs)  42.1 us
    mul x15, local copies, waits for them, and re-layouts, backward_layer(): gate_now[:, :, None] * d_wide[:, None, :]  41 us
    ppermute x8, starting transfers between devices, passed_along(): return lax.ppermute(shard, axis, pairs)  39.3 us
    all_to_all x1, blocking collectives, backward_layer(): lax.all_to_all(outbound, 'expert', split_axis=0, concat_axis=0, tiled=True)  37.8 us
  transfers between devices with their start and end apart: 27, of which 27 were waited for; matrix products, arithmetic and copies ran while one was open for 9% of the time, Pallas kernels for 0%

commit v1 on v0

v1 whole, which is shorter than its diff:
```python
import jax
import jax.numpy as jnp
from jax import lax
from jax.sharding import PartitionSpec as P

TOP = 6

epsilon = 1e-06


def exchange(rows):
    feat = rows.shape[1]
    peers = lax.axis_size("expert")
    blocks = rows.reshape(peers, -1, feat)
    moved = lax.all_to_all(blocks, "expert", split_axis=0, concat_axis=0, tiled=True)
    return moved.reshape(rows.shape)


def slot_matrices(route_block, gate_block, experts, capacity):
    flat_ids = route_block.reshape(-1)
    count = flat_ids.shape[0]
    onehot = flat_ids[:, None] == jnp.arange(experts, dtype=jnp.int32)[None, :]
    order = jnp.arange(count, dtype=jnp.int32)
    earlier = (order[:, None] > order[None, :]).astype(jnp.bfloat16)
    before = jnp.dot(
        earlier, onehot.astype(jnp.bfloat16), preferred_element_type=jnp.float32
    )
    position = jnp.sum(jnp.where(onehot, before, 0.0), axis=1).astype(jnp.int32)
    slots = (flat_ids * capacity + position).reshape(route_block.shape)
    places = jnp.arange(experts * capacity, dtype=jnp.int32)
    hit = slots[:, :, None] == places[None, None, :]
    picks = jnp.sum(hit.astype(jnp.float32), axis=1)
    weights = jnp.sum(jnp.where(hit, gate_block[:, :, None], 0.0), axis=1)
    return picks.astype(jnp.bfloat16), weights


def spread(picks, rows):
    return lax.dot_general(
        picks, rows, (((0,), (0,)), ((), ())), preferred_element_type=jnp.float32
    )


def gathered_sum(weights, rows):
    high = lax.reduce_precision(weights, 8, 7)
    both = jnp.concatenate([high, weights - high], axis=0).astype(jnp.bfloat16)
    parts = jnp.dot(both, rows, preferred_element_type=jnp.float32)
    half = weights.shape[0]
    return parts[:half] + parts[half:]


def inverse_rms(wide_in):
    return lax.rsqrt(jnp.mean(wide_in * wide_in, axis=1, keepdims=True) + epsilon)


def normed_rows(layer_in, gain):
    wide_in = layer_in.astype(jnp.float32)
    return (wide_in * inverse_rms(wide_in) * gain).astype(jnp.bfloat16)


def hidden_forward(rows, gate_mat, up_mat):
    gate_pre = jnp.dot(rows, gate_mat, preferred_element_type=jnp.float32)
    up_val = jnp.dot(rows, up_mat, preferred_element_type=jnp.float32)
    activated = (jax.nn.silu(gate_pre) * up_val).astype(jnp.bfloat16)
    return activated, gate_pre, up_val


def project_down(activated, down_mat):
    return jnp.dot(activated, down_mat, preferred_element_type=jnp.float32).astype(jnp.bfloat16)


CONTRACT = (((1,), (1,)), ((), ()))


def hidden_grad(d_rows, down_mat):
    return lax.dot_general(d_rows, down_mat, CONTRACT, preferred_element_type=jnp.float32)


def rows_grad(d_act, gate_pre, up_val, gate_mat, up_mat):
    sigmoid_g = jax.nn.sigmoid(gate_pre)
    d_gate = (d_act * up_val * sigmoid_g * (1.0 + gate_pre * (1.0 - sigmoid_g))).astype(
        jnp.bfloat16
    )
    d_up = (d_act * gate_pre * sigmoid_g).astype(jnp.bfloat16)
    summed = lax.dot_general(d_gate, gate_mat, CONTRACT, preferred_element_type=jnp.float32)
    summed = summed + lax.dot_general(d_up, up_mat, CONTRACT, preferred_element_type=jnp.float32)
    return summed.astype(jnp.bfloat16)


def layer_grad(dy, layer_in, gain, picks, returned):
    wide_in = layer_in.astype(jnp.float32)
    inv_rms = inverse_rms(wide_in)
    d_norm = jnp.dot(picks, returned, preferred_element_type=jnp.float32)
    scaled = gain * d_norm
    inner = jnp.mean(wide_in * scaled, axis=1, keepdims=True)
    cubed = inv_rms * inv_rms * inv_rms
    return (dy.astype(jnp.float32) + inv_rms * scaled - wide_in * cubed * inner).astype(
        jnp.bfloat16
    )


def local(inputs, cotangent, norm_gain, routes, route_gates, w_gate, w_up, w_down):
    segment_id = lax.axis_index("segment")
    experts = lax.axis_size("expert") * w_gate.shape[1]
    micro_count, tok_rows, feat_width = inputs.shape
    capacity = min(tok_rows, 4 * tok_rows * TOP // (3 * experts))
    hidden = w_gate.shape[3]
    slots = experts * capacity
    mine = segment_id % 2
    early = segment_id < 2
    swap = [(0, 1), (1, 0), (2, 3), (3, 2)]

    def swapped(value):
        return lax.ppermute(value, "segment", swap)

    def ordered(own, other):
        low = jnp.where(mine == 0, own, other)
        high = jnp.where(mine == 0, other, own)
        return low, high

    def of_micro(value, which):
        return lax.dynamic_index_in_dim(value, which, 0, keepdims=False)

    own_mats = (w_gate[0, 0], w_up[0, 0], w_down[0, 0])
    route_low, route_high = ordered(
        of_micro(routes[0], mine), swapped(of_micro(routes[0], 1 - mine))
    )
    gate_low, gate_high = ordered(
        of_micro(route_gates[0], mine), swapped(of_micro(route_gates[0], 1 - mine))
    )
    gain_low, gain_high = ordered(norm_gain, swapped(norm_gain))
    other_mats = tuple(swapped(mat) for mat in own_mats)

    def with_mats(level, run, *values):
        return lax.cond(
            mine == level,
            lambda held: run(held, own_mats),
            lambda held: run(held, other_mats),
            values,
        )

    picks_low, mix_low = slot_matrices(route_low, gate_low, experts, capacity)
    picks_high, mix_high = slot_matrices(route_high, gate_high, experts, capacity)
    scale_low = jnp.sum(mix_low, axis=0)[:, None]
    scale_high = jnp.sum(mix_high, axis=0)[:, None]

    first_in = of_micro(inputs, mine)
    last_grad = of_micro(cotangent, mine)
    source = jnp.where(early, normed_rows(first_in, gain_low), last_grad)
    picks_first = jnp.where(early, picks_low, picks_high)
    scale_first = jnp.where(early, 1.0, scale_high)
    arrived = exchange((scale_first * spread(picks_first, source)).astype(jnp.bfloat16))

    def send_rows(layer_in, gain, picks):
        return exchange(spread(picks, normed_rows(layer_in, gain)).astype(jnp.bfloat16))

    def send_grads(dy, picks, scale):
        return exchange((scale * spread(picks, dy)).astype(jnp.bfloat16))

    def run_forward(held, mats):
        activated, gate_pre, up_val = hidden_forward(held[0], mats[0], mats[1])
        return project_down(activated, mats[2]), gate_pre, up_val

    def mixed(layer_in, mix, returned):
        return (layer_in.astype(jnp.float32) + gathered_sum(mix, returned)).astype(jnp.bfloat16)

    def run_backward(held, mats):
        d_rows, gate_pre, up_val = held
        return rows_grad(hidden_grad(d_rows, mats[2]), gate_pre, up_val, mats[0], mats[1])

    def run_joint(held, mats):
        rows, d_act = held
        activated, gate_pre, up_val = hidden_forward(rows, mats[0], mats[1])
        return activated, rows_grad(d_act, gate_pre, up_val, mats[0], mats[1])

    no_rows = jnp.zeros((tok_rows, feat_width), jnp.bfloat16)
    no_hidden = jnp.zeros((slots, hidden), jnp.float32)

    def climb(got):
        out_low, pre_low, up_low = with_mats(0, run_forward, got)
        state_low = mixed(first_in, mix_low, exchange(out_low))
        got_high = send_rows(state_low, gain_high, picks_high)
        out_high, pre_high, up_high = with_mats(1, run_forward, got_high)
        state_high = mixed(state_low, mix_high, exchange(out_high))
        return state_low, state_high, pre_low, up_low, pre_high, up_high

    def prepare(got):
        d_act = with_mats(1, lambda held, mats: hidden_grad(held[0], mats[2]), got)
        return no_rows, no_rows, d_act, no_hidden, no_hidden, no_hidden

    state_low, state_high, kept_a, kept_b, kept_c, kept_d = lax.cond(
        early, climb, prepare, arrived
    )
    relayed = lax.ppermute(state_high, "segment", [(0, 2), (1, 3)])

    def turn(held):
        layer_in, d_act = held
        got_low = send_rows(layer_in, gain_low, picks_low)
        out_low, pre_low, up_low = with_mats(0, run_forward, got_low)
        state = mixed(layer_in, mix_low, exchange(out_low))
        got_high = send_rows(state, gain_high, picks_high)
        activated, d_rows = with_mats(1, run_joint, got_high, d_act)
        grad_high = layer_grad(last_grad, state, gain_high, picks_high, exchange(d_rows))
        d_got = send_grads(grad_high, picks_low, scale_low)
        d_rows_low = with_mats(0, run_backward, d_got, pre_low, up_low)
        grad_low = layer_grad(grad_high, layer_in, gain_low, picks_low, exchange(d_rows_low))
        return state, activated, grad_high, grad_low

    def stay(held):
        return no_rows, jnp.zeros((slots, hidden), jnp.bfloat16), no_rows, no_rows

    turn_state, activated, turn_high, turn_low = lax.cond(early, stay, turn, (relayed, kept_a))
    came_back = lax.ppermute(turn_low, "segment", [(2, 0), (3, 1)])

    def descend(dy):
        d_got = send_grads(dy, picks_high, scale_high)
        d_rows_high = with_mats(1, run_backward, d_got, kept_c, kept_d)
        grad_high = layer_grad(dy, state_low, gain_high, picks_high, exchange(d_rows_high))
        d_got_low = send_grads(grad_high, picks_low, scale_low)
        d_rows_low = with_mats(0, run_backward, d_got_low, kept_a, kept_b)
        grad_low = layer_grad(grad_high, first_in, gain_low, picks_low, exchange(d_rows_low))
        return state_low, state_high, grad_low, grad_high

    def finish(dy):
        out_high = with_mats(1, lambda held, mats: project_down(held[0], mats[2]), activated)
        state = mixed(turn_state, mix_high, exchange(out_high))
        return turn_state, state, turn_low, turn_high

    end_low, end_high, back_low, back_high = lax.cond(early, descend, finish, came_back)
    kept = jnp.where(
        mine == 0, jnp.stack([end_low, back_low]), jnp.stack([end_high, back_high])
    )
    given = jnp.where(
        mine == 0, jnp.stack([end_high, back_high]), jnp.stack([end_low, back_low])
    )
    taken = swapped(given)
    first = jnp.where(mine == 0, kept, taken)
    second = jnp.where(mine == 0, taken, kept)
    return (
        jnp.stack([first[0], second[0]])[None],
        jnp.stack([first[1], second[1]])[None],
    )


def solution(mesh):
    placed = (
        P(None, "expert", None),
        P(None, "expert", None),
        P("segment", None),
        P("segment", None, "expert", None),
        P("segment", None, "expert", None),
        P("segment", "expert", None, None),
        P("segment", "expert", None, None),
        P("segment", "expert", None, None),
    )
    return jax.shard_map(
        local,
        mesh=mesh,
        in_specs=placed,
        out_specs=(P("segment", None, "expert", None), P("segment", None, "expert", None)),
        check_vma=False,
    )
```

time: 1180 us -> 804 us (0.68); the launches traced: 1160 us -> 801 us
  local copies, waits for them, and re-layouts: 244 us -> 11.4 us
  other arithmetic: 125 us -> 25.9 us
  starting transfers between devices: 172 us -> 77.9 us
  waiting for transfers between devices: 528 us -> 582 us
  blocking collectives: 37.8 us -> 0 us
  matrix products: 48.1 us -> 82.7 us
  loops' own time: 1.25 us -> 20.4 us
    ppermute x8 -> x9, waiting for transfers between devices: 42.1 us -> 325 us  [the longest x1 319 us: local(): came_back = lax.ppermute(turn_low, 'segment', [(2, 0), (3, 1)])]
    all_to_all x19 -> x8, waiting for transfers between devices: 486 us -> 256 us  [exchange(): lax.all_to_all(blocks, 'expert', split_axis=0, concat_axis=0, tiled=True)]
    all_to_all x19 -> x8, starting transfers between devices: 132 us -> 72.3 us  [exchange(): lax.all_to_all(blocks, 'expert', split_axis=0, concat_axis=0, tiled=True)]
    reduce_sum x30 -> x3, other arithmetic: 49.4 us -> 3.26 us  [the longest x2 2.2 us: inverse_rms(): jnp.mean(wide_in * wide_in, axis=1, keepdims=True) + epsilon]
    mul x30 -> x0, local copies, waits for them, and re-layouts: 43.5 us -> none  [the longest x15 41 us: backward_layer(): gate_now[:, :, None] * d_wide[:, None, :]]
    convert_element_type x10 -> x4, local copies, waits for them, and re-layouts: 43.4 us -> 0.4 us  [slot_matrices(): position = jnp.sum(jnp.where(onehot, before, 0.0), axis=1).astype(jnp.int32)]
    all_to_all x1 -> x0, blocking collectives: 37.8 us -> none  [backward_layer(): lax.all_to_all(outbound, 'expert', split_axis=0, concat_axis=0, tiled=True)]
    gather x10 -> x0, local copies, waits for them, and re-layouts: 36.9 us -> none  [the longest x5 20.4 us: backward_layer(): returned.reshape(-1, feat_width)[slot_ids].astype(jnp.float32)]
  transfers between devices with their start and end apart: 27 -> 17, of which waited for: 27 -> 11; matrix products, arithmetic and copies ran while one was open for 9% -> 1% of each run, Pallas kernels for 0% -> 0%
where the time goes in v1:
time: 804 us; the launch traced here: 801 us
  waiting for transfers between devices  582 us (72%)
  matrix products  82.7 us (10%)
  starting transfers between devices  77.9 us (10%)
  other arithmetic  25.9 us (3%)
  loops' own time  20.4 us (3%)
  local copies, waits for them, and re-layouts  11.4 us (1%)
    ppermute x1, waiting for transfers between devices, local(): came_back = lax.ppermute(turn_low, 'segment', [(2, 0), (3, 1)])  319 us
    all_to_all x8, waiting for transfers between devices, exchange(): lax.all_to_all(blocks, 'expert', split_axis=0, concat_axis=0, tiled=True)  256 us
    all_to_all x8, starting transfers between devices, exchange(): lax.all_to_all(blocks, 'expert', split_axis=0, concat_axis=0, tiled=True)  72.3 us
  transfers between devices with their start and end apart: 17, of which 11 were waited for; matrix products, arithmetic and copies ran while one was open for 1% of the time, Pallas kernels for 0%

profile of v1, /device:TPU:1, one launch (start us, length us, event | category | flops | bytes accessed | tf_op | source)
XLA Modules:
  0.0 800.9 jit_solution(14157837937591593935)
XLA Ops:
  10.0 2.4 multiply_convert_fusion.47
  12.4 10.6 %all-to-all-start.14 = ((bf16[32,16,2560]{2,1,0:T(8,128)(2,1)}), bf16[32,16,2560]{2,1,0:T(8,128)(2,1)S(1)}, u32[]{:S(2)}, u32[]{:S(2)}) async-start(bf16[32,16,2560]{2,1,0:T(8,128)(2,1)} %bitcast.47), calls=%async_computation.14 | async-start | bytes 5242880 | tf_op jit(solution)/shard_map/all_to_all | solution.py:15
  23.0 32.8 %all-to-all-done.14 = bf16[32,16,2560]{2,1,0:T(8,128)(2,1)S(1)} async-done(((bf16[32,16,2560]{2,1,0:T(8,128)(2,1)}), bf16[32,16,2560]{2,1,0:T(8,128)(2,1)S(1)}, u32[]{:S(2)}, u32[]{:S(2)}) %all-to-all-start.14) | async-done | bytes 2621472 | tf_op jit(solution)/shard_map/all_to_all | solution.py:15
  55.9 170.8 %conditional.33 = (bf16[64,2560]{1,0:T(8,128)(2,1)}, bf16[64,2560]{1,0:T(8,128)(2,1)S(1)}, f32[512,768]{1,0:T(8,128)}, f32[512,768]{1,0:T(8,128)}, f32[512,768]{1,0:T(8,128)}, /*index=5*/f32[512,768]{1,0:T(8,128)}) conditional(s32[]{:T(128)} %convert_element_type.292, (s32[]{:T(128)}, bf16[512,2560]{1,0:T(8,128)(2,1)S(1)}, ...), branch_computations={%region_8.11_spmd, %region_11.17_spmd} | conditional | flops 12927729664 | bytes 175537712 | solution.py:190
  55.9 28.2 %conditional.10 = (bf16[512,2560]{1,0:T(8,128)(2,1)S(1)}, f32[512,768]{1,0:T(8,128)}, f32[512,768]{1,0:T(8,128)}) conditional(s32[]{:T(128)} %convert_element_type.214, (bf16[512,2560]{1,0:T(8,128)(2,1)S(1)}, bf16[2560,768]{1,0:T(8,128)(2,1)}, bf16[2560,768]{1,0:T(8,128)(2,1)}, bf16[768,2560]{1,0:T(8,128)(2,1)}) %tuple.104, ...), branch_computations={%region_12.12_spmd, %region_13.13_spmd} | conditional | flops 6042157056 | bytes 57409616
  55.9 5.5 fusion.164
  61.4 5.5 fusion.165
  66.9 5.3 fusion
  85.6 8.7 %all-to-all-start = ((bf16[32,16,2560]{2,1,0:T(8,128)(2,1)}), bf16[32,16,2560]{2,1,0:T(8,128)(2,1)S(1)}, u32[]{:S(2)}, u32[]{:S(2)}) async-start(bf16[32,16,2560]{2,1,0:T(8,128)(2,1)} %bitcast.213), calls=%async_computation | async-start | bytes 5242880 | tf_op jit(solution)/shard_map/cond/branch_1_fun/all_to_all | solution.py:15
  94.4 33.0 %all-to-all-done = bf16[32,16,2560]{2,1,0:T(8,128)(2,1)S(1)} async-done(((bf16[32,16,2560]{2,1,0:T(8,128)(2,1)}), bf16[32,16,2560]{2,1,0:T(8,128)(2,1)S(1)}, u32[]{:S(2)}, u32[]{:S(2)}) %all-to-all-start) | async-done | bytes 2621472 | tf_op jit(solution)/shard_map/cond/branch_1_fun/all_to_all | solution.py:15
  128.9 3.4 convolution_convert_fusion
  132.2 6.6 all-to-all-start.1
  138.8 32.4 %all-to-all-done.1 = bf16[32,16,2560]{2,1,0:T(8,128)(2,1)S(1)} async-done(((bf16[32,16,2560]{2,1,0:T(8,128)(2,1)}), bf16[32,16,2560]{2,1,0:T(8,128)(2,1)S(1)}, u32[]{:S(2)}, u32[]{:S(2)}) %all-to-all-start.1) | async-done | bytes 2621472 | tf_op jit(solution)/shard_map/cond/branch_1_fun/all_to_all | solution.py:15
  171.2 13.1 %conditional.11 = (bf16[512,2560]{1,0:T(8,128)(2,1)S(1)}, f32[512,768]{1,0:T(8,128)}, f32[512,768]{1,0:T(8,128)}) conditional(s32[]{:T(128)} %convert_element_type.218, (bf16[512,2560]{1,0:T(8,128)(2,1)S(1)}, bf16[2560,768]{1,0:T(8,128)(2,1)}, bf16[2560,768]{1,0:T(8,128)(2,1)}, bf16[768,2560]{1,0:T(8,128)(2,1)}) %tuple.222, ...), branch_computations={%region_15.15_spmd, %region_16.16_spmd} | conditional | flops 6042157056 | bytes 57409616
  171.2 5.6 fusion.170
  176.9 3.4 fusion.171
  180.2 4.1 fusion.9
  185.9 8.7 %all-to-all-start.2 = ((bf16[32,16,2560]{2,1,0:T(8,128)(2,1)}), bf16[32,16,2560]{2,1,0:T(8,128)(2,1)S(1)}, u32[]{:S(2)}, u32[]{:S(2)}) async-start(bf16[32,16,2560]{2,1,0:T(8,128)(2,1)} %bitcast.214), calls=%async_computation.2 | async-start | bytes 5242880 | tf_op jit(solution)/shard_map/cond/branch_1_fun/all_to_all | solution.py:15
  194.6 30.0 %all-to-all-done.2 = bf16[32,16,2560]{2,1,0:T(8,128)(2,1)S(1)} async-done(((bf16[32,16,2560]{2,1,0:T(8,128)(2,1)}), bf16[32,16,2560]{2,1,0:T(8,128)(2,1)S(1)}, u32[]{:S(2)}, u32[]{:S(2)}) %all-to-all-start.2) | async-done | bytes 2621472 | tf_op jit(solution)/shard_map/cond/branch_1_fun/all_to_all | solution.py:15
  228.7 4.3 collective-permute-done.6
  233.0 8.7 %conditional.34 = (bf16[64,2560]{1,0:T(8,128)(2,1)S(1)}, bf16[512,768]{1,0:T(8,128)(2,1)}, bf16[64,2560]{1,0:T(8,128)(2,1)}, bf16[64,2560]{1,0:T(8,128)(2,1)S(1)}) conditional(s32[]{:T(128)} %convert_element_type.292, (bf16[64,2560]{1,0:T(8,128)(2,1)S(1)}, f32[64,512]{1,0:T(8,128)}, s32[]{:T(128)}, f32[1,2560]{1,0:T(1,128)}, ...), branch_computations={%region_18.29_spmd, %region_29.30_spmd} | conditional | flops 21342126080 | bytes 389610240 | solution.py:211
  243.0 319.3 %collective-permute-done.7 = bf16[64,2560]{1,0:T(8,128)(2,1)S(1)} collective-permute-done((bf16[64,2560]{1,0:T(8,128)(2,1)S(1)}, bf16[64,2560]{1,0:T(8,128)(2,1)S(1)}, u32[]{:S(2)}, u32[]{:S(2)}) %collective-permute-start.7) | collective-permute-done | bytes 327712 | tf_op jit(solution)/shard_map/ppermute | solution.py:212
  562.3 231.7 %conditional.35 = (bf16[64,2560]{1,0:T(8,128)(2,1)S(1)}, bf16[64,2560]{1,0:T(8,128)(2,1)}, bf16[64,2560]{1,0:T(8,128)(2,1)}, bf16[1,64,2560]{2,1,0:T(8,128)(2,1)}) conditional(s32[]{:T(128)} %convert_element_type.292, (bf16[64,2560]{1,0:T(8,128)(2,1)S(1)}, f32[64,512]{1,0:T(8,128)S(1)}, s32[]{:T(128)}, bf16[512,768]{1,0:T(8,128)(2,1)}, ...), branch_computations={%region_30.33_spmd, %region_33.42_spmd} | conditional | flops 12778340352 | bytes 209958496 | solution.py:228
  562.3 3.1 multiply_convert_fusion.46
  565.4 7.8 all-to-all-start.10
  573.2 32.1 %all-to-all-done.10 = bf16[32,16,2560]{2,1,0:T(8,128)(2,1)S(1)} async-done(((bf16[32,16,2560]{2,1,0:T(8,128)(2,1)}), bf16[32,16,2560]{2,1,0:T(8,128)(2,1)S(1)}, u32[]{:S(2)}, u32[]{:S(2)}) %all-to-all-start.10) | async-done | bytes 2621472 | tf_op jit(solution)/shard_map/cond/branch_1_fun/all_to_all | solution.py:15
  605.2 18.1 %conditional.28 = (f32[512,2560]{1,0:T(8,128)}, f32[512,2560]{1,0:T(8,128)}) conditional(s32[]{:T(128)} %convert_element_type.269, (bf16[512,2560]{1,0:T(8,128)(2,1)S(1)}, bf16[768,2560]{1,0:T(8,128)(2,1)}, f32[512,768]{1,0:T(8,128)}, f32[512,768]{1,0:T(8,128)}, bf16[2560,768]{1,0:T(8,128)(2,1)}, ...), branch_computations={%region_35.35_spmd, %region_36.36_spmd} | conditional | flops 6046089216 | bytes 65798216
  605.6 4.5 fusion.181
  610.1 7.0 fusion.57
  617.2 6.1 fusion.58
  623.3 6.2 add_convert_fusion.3
  629.5 9.1 %all-to-all-start.11 = ((bf16[32,16,2560]{2,1,0:T(8,128)(2,1)}), bf16[32,16,2560]{2,1,0:T(8,128)(2,1)S(1)}, u32[]{:S(2)}, u32[]{:S(2)}) async-start(bf16[32,16,2560]{2,1,0:T(8,128)(2,1)} %bitcast.194), calls=%async_computation.11 | async-start | bytes 5242880 | tf_op jit(solution)/shard_map/cond/branch_1_fun/all_to_all | solution.py:15
  638.7 30.1 %all-to-all-done.11 = bf16[32,16,2560]{2,1,0:T(8,128)(2,1)S(1)} async-done(((bf16[32,16,2560]{2,1,0:T(8,128)(2,1)}), bf16[32,16,2560]{2,1,0:T(8,128)(2,1)S(1)}, u32[]{:S(2)}, u32[]{:S(2)}) %all-to-all-start.11) | async-done | bytes 2621472 | tf_op jit(solution)/shard_map/cond/branch_1_fun/all_to_all | solution.py:15
  668.8 1.7 fusion.127
  670.5 2.0 fusion.130
  672.5 3.4 multiply_convert_fusion.45
  675.9 11.5 %all-to-all-start.12 = ((bf16[32,16,2560]{2,1,0:T(8,128)(2,1)}), bf16[32,16,2560]{2,1,0:T(8,128)(2,1)S(1)}, u32[]{:S(2)}, u32[]{:S(2)}) async-start(bf16[32,16,2560]{2,1,0:T(8,128)(2,1)} %bitcast.35), calls=%async_computation.12 | async-start | bytes 5242880 | tf_op jit(solution)/shard_map/cond/branch_1_fun/all_to_all | solution.py:15
  687.4 32.1 %all-to-all-done.12 = bf16[32,16,2560]{2,1,0:T(8,128)(2,1)S(1)} async-done(((bf16[32,16,2560]{2,1,0:T(8,128)(2,1)}), bf16[32,16,2560]{2,1,0:T(8,128)(2,1)S(1)}, u32[]{:S(2)}, u32[]{:S(2)}) %all-to-all-start.12) | async-done | bytes 2621472 | tf_op jit(solution)/shard_map/cond/branch_1_fun/all_to_all | solution.py:15
  719.6 19.9 %conditional.29 = (f32[512,2560]{1,0:T(8,128)}, f32[512,2560]{1,0:T(8,128)}) conditional(s32[]{:T(128)} %convert_element_type.275, (bf16[512,2560]{1,0:T(8,128)(2,1)S(1)}, bf16[768,2560]{1,0:T(8,128)(2,1)}, f32[512,768]{1,0:T(8,128)}, f32[512,768]{1,0:T(8,128)}, bf16[2560,768]{1,0:T(8,128)(2,1)}, ...), branch_computations={%region_39.39_spmd, %region_40.40_spmd} | conditional | flops 6046089216 | bytes 65798216
  719.7 4.3 fusion.182
  724.1 8.1 %fusion.63 = f32[512,2560]{1,0:T(8,128)} fusion(bf16[2560,768]{1,0:T(8,128)(2,1)} %get-tuple-element.448, f32[512,768]{1,0:T(8,128)} %get-tuple-element.447, f32[512,768]{1,0:T(8,128)S(1)} %fusion.182, f32[512,768]{1,0:T(8,128)} %get-tuple-element.446), kind=kOutput, calls=%fused_computation.95 | convolution fusion | flops 2017198080 | bytes 13893632 | tf_op jit(solution)/shard_map/cond/branch_1_fun/cond/branch_0_fun/dot_general | solution.py:84
  732.2 7.3 fusion.64
  739.4 6.2 add_convert_fusion.2
  745.7 9.2 %all-to-all-start.13 = ((bf16[32,16,2560]{2,1,0:T(8,128)(2,1)}), bf16[32,16,2560]{2,1,0:T(8,128)(2,1)S(1)}, u32[]{:S(2)}, u32[]{:S(2)}) async-start(bf16[32,16,2560]{2,1,0:T(8,128)(2,1)} %bitcast.193), calls=%async_computation.13 | async-start | bytes 5242880 | tf_op jit(solution)/shard_map/cond/branch_1_fun/all_to_all | solution.py:15
  755.9 1.7 copy.121
  757.6 33.5 %all-to-all-done.13 = bf16[32,16,2560]{2,1,0:T(8,128)(2,1)S(1)} async-done(((bf16[32,16,2560]{2,1,0:T(8,128)(2,1)}), bf16[32,16,2560]{2,1,0:T(8,128)(2,1)S(1)}, u32[]{:S(2)}, u32[]{:S(2)}) %all-to-all-start.13) | async-done | bytes 2621472 | tf_op jit(solution)/shard_map/cond/branch_1_fun/all_to_all | solution.py:15
  791.8 2.0 fusion.135
  795.6 1.9 collective-permute-done.8
  (106 shorter events, 26.9 us)
Async XLA Ops:
  0.6 4.2 copy-start
  0.6 8.7 %copy-start.29 = (f32[1,2560]{1,0:T(1,128)S(1)}, f32[1,2560]{1,0:T(1,128)}, u32[]{:S(2)}) copy-start(f32[1,2560]{1,0:T(1,128)} %param.34) | copy-start | bytes 30724
  1.5 6.2 collective-permute-start.1
  3.7 2.4 collective-permute-start
  3.8 5.6 collective-permute-start.2
  4.3 51.5 %collective-permute-start.4 = (bf16[2560,768]{1,0:T(8,128)(2,1)}, bf16[2560,768]{1,0:T(8,128)(2,1)}, u32[]{:S(2)}, u32[]{:S(2)}) collective-permute-start(bf16[2560,768]{1,0:T(8,128)(2,1)} %bitcast.230), channel_id=1, source_target_pairs={{0,32},{32,0},{64,96},{96,64},{1,33},{33,1},{65,97},{97,65},{2,34}... | collective-permute-start | bytes 11796488 | tf_op jit(solution)/shard_map/ppermute | solution.py:113
  4.4 51.5 %collective-permute-start.5 = (bf16[2560,768]{1,0:T(8,128)(2,1)}, bf16[2560,768]{1,0:T(8,128)(2,1)}, u32[]{:S(2)}, u32[]{:S(2)}) collective-permute-start(bf16[2560,768]{1,0:T(8,128)(2,1)} %bitcast.234), channel_id=1, source_target_pairs={{0,32},{32,0},{64,96},{96,64},{1,33},{33,1},{65,97},{97,65},{2,34}... | collective-permute-start | bytes 11796488 | tf_op jit(solution)/shard_map/ppermute | solution.py:113
  4.8 7.6 copy-start.10
  6.1 49.7 %copy-start.2 = (bf16[64,2560]{1,0:T(8,128)(2,1)}, bf16[64,2560]{1,0:T(8,128)(2,1)S(1)}, u32[]{:S(2)}) copy-start(bf16[64,2560]{1,0:T(8,128)(2,1)S(1)} %get-tuple-element.531) | copy-start | bytes 983044
  6.2 49.7 %collective-permute-start.3 = (bf16[768,2560]{1,0:T(8,128)(2,1)}, bf16[768,2560]{1,0:T(8,128)(2,1)}, u32[]{:S(2)}, u32[]{:S(2)}) collective-permute-start(bf16[768,2560]{1,0:T(8,128)(2,1)} %bitcast.224), channel_id=1, source_target_pairs={{0,32},{32,0},{64,96},{96,64},{1,33},{33,1},{65,97},{97,65},{2,34}... | collective-permute-start | bytes 11796488 | tf_op jit(solution)/shard_map/ppermute | solution.py:113
  8.8 0.6 copy-start.28
  12.4 43.4 %all-to-all-start.14 = ((bf16[32,16,2560]{2,1,0:T(8,128)(2,1)}), bf16[32,16,2560]{2,1,0:T(8,128)(2,1)S(1)}, u32[]{:S(2)}, u32[]{:S(2)}) async-start(bf16[32,16,2560]{2,1,0:T(8,128)(2,1)} %bitcast.47), calls=%async_computation.14 | async-start | bytes 5242880 | tf_op jit(solution)/shard_map/all_to_all | solution.py:15
  84.1 1.5 copy-start.14
  85.6 8.7 %copy-start.21 = (f32[64,512]{1,0:T(8,128)S(1)}, f32[64,512]{1,0:T(8,128)}, u32[]{:S(2)}) copy-start(f32[64,512]{1,0:T(8,128)} %get-tuple-element.350) | copy-start | bytes 393220 | tf_op jit(solution)/shard_map/cond
  85.6 41.8 %all-to-all-start = ((bf16[32,16,2560]{2,1,0:T(8,128)(2,1)}), bf16[32,16,2560]{2,1,0:T(8,128)(2,1)S(1)}, u32[]{:S(2)}, u32[]{:S(2)}) async-start(bf16[32,16,2560]{2,1,0:T(8,128)(2,1)} %bitcast.213), calls=%async_computation | async-start | bytes 5242880 | tf_op jit(solution)/shard_map/cond/branch_1_fun/all_to_all | solution.py:15
  132.2 39.0 %all-to-all-start.1 = ((bf16[32,16,2560]{2,1,0:T(8,128)(2,1)}), bf16[32,16,2560]{2,1,0:T(8,128)(2,1)S(1)}, u32[]{:S(2)}, u32[]{:S(2)}) async-start(bf16[32,16,2560]{2,1,0:T(8,128)(2,1)} %bitcast.3), calls=%async_computation.1 | async-start | bytes 5242880 | tf_op jit(solution)/shard_map/cond/branch_1_fun/all_to_all | solution.py:15
  171.2 5.6 copy-start.45
  176.9 3.4 copy-start.37
  184.3 1.5 copy-start.15
  185.9 38.8 %all-to-all-start.2 = ((bf16[32,16,2560]{2,1,0:T(8,128)(2,1)}), bf16[32,16,2560]{2,1,0:T(8,128)(2,1)S(1)}, u32[]{:S(2)}, u32[]{:S(2)}) async-start(bf16[32,16,2560]{2,1,0:T(8,128)(2,1)} %bitcast.214), calls=%async_computation.2 | async-start | bytes 5242880 | tf_op jit(solution)/shard_map/cond/branch_1_fun/all_to_all | solution.py:15
  226.7 0.7 copy-start.20
  227.4 5.6 collective-permute-start.6
  233.0 329.3 %copy-start.3 = (bf16[64,2560]{1,0:T(8,128)(2,1)S(1)}, bf16[64,2560]{1,0:T(8,128)(2,1)}, u32[]{:S(2)}) copy-start(bf16[64,2560]{1,0:T(8,128)(2,1)} %copy-done.2) | copy-start | bytes 983044
  241.7 320.6 %copy-start.12 = (bf16[64,2560]{1,0:T(8,128)(2,1)}, bf16[64,2560]{1,0:T(8,128)(2,1)S(1)}, u32[]{:S(2)}) copy-start(bf16[64,2560]{1,0:T(8,128)(2,1)S(1)} %get-tuple-element.501) | copy-start | bytes 983044
  241.7 320.6 %collective-permute-start.7 = (bf16[64,2560]{1,0:T(8,128)(2,1)S(1)}, bf16[64,2560]{1,0:T(8,128)(2,1)S(1)}, u32[]{:S(2)}, u32[]{:S(2)}) collective-permute-start(bf16[64,2560]{1,0:T(8,128)(2,1)S(1)} %get-tuple-element.501), channel_id=1, source_target_pairs={{64,0},{96,32},{65,1},{97,33},{66,2},{98,34},{67,3},{99,35},{68,4}... | collective-permute-start | bytes 983048 | tf_op jit(solution)/shard_map/ppermute | solution.py:212
  562.3 3.1 copy-start.18
  565.4 39.9 %all-to-all-start.10 = ((bf16[32,16,2560]{2,1,0:T(8,128)(2,1)}), bf16[32,16,2560]{2,1,0:T(8,128)(2,1)S(1)}, u32[]{:S(2)}, u32[]{:S(2)}) async-start(bf16[32,16,2560]{2,1,0:T(8,128)(2,1)} %bitcast.28), calls=%async_computation.10 | async-start | bytes 5242880 | tf_op jit(solution)/shard_map/cond/branch_1_fun/all_to_all | solution.py:15
  605.6 4.5 copy-start.42
  610.1 7.0 copy-start.49
  629.5 39.3 %all-to-all-start.11 = ((bf16[32,16,2560]{2,1,0:T(8,128)(2,1)}), bf16[32,16,2560]{2,1,0:T(8,128)(2,1)S(1)}, u32[]{:S(2)}, u32[]{:S(2)}) async-start(bf16[32,16,2560]{2,1,0:T(8,128)(2,1)} %bitcast.194), calls=%async_computation.11 | async-start | bytes 5242880 | tf_op jit(solution)/shard_map/cond/branch_1_fun/all_to_all | solution.py:15
  668.8 1.7 copy-start.19
  675.9 43.7 %all-to-all-start.12 = ((bf16[32,16,2560]{2,1,0:T(8,128)(2,1)}), bf16[32,16,2560]{2,1,0:T(8,128)(2,1)S(1)}, u32[]{:S(2)}, u32[]{:S(2)}) async-start(bf16[32,16,2560]{2,1,0:T(8,128)(2,1)} %bitcast.35), calls=%async_computation.12 | async-start | bytes 5242880 | tf_op jit(solution)/shard_map/cond/branch_1_fun/all_to_all | solution.py:15
  745.7 10.2 %copy-start.27 = (f32[1,2560]{1,0:T(1,128)S(1)}, f32[1,2560]{1,0:T(1,128)}, u32[]{:S(2)}) copy-start(f32[1,2560]{1,0:T(1,128)} %get-tuple-element.473) | copy-start | bytes 30724 | tf_op jit(solution)/shard_map/cond
  745.7 45.5 %all-to-all-start.13 = ((bf16[32,16,2560]{2,1,0:T(8,128)(2,1)}), bf16[32,16,2560]{2,1,0:T(8,128)(2,1)S(1)}, u32[]{:S(2)}, u32[]{:S(2)}) async-start(bf16[32,16,2560]{2,1,0:T(8,128)(2,1)} %bitcast.193), calls=%async_computation.13 | async-start | bytes 5242880 | tf_op jit(solution)/shard_map/cond/branch_1_fun/all_to_all | solution.py:15
  794.0 3.5 copy-start.13
  795.4 2.2 collective-permute-start.8
  798.8 1.9 copy-start.1

commit v2 on v1

--- a/solution.py
+++ b/solution.py
@@ -1,11 +1,326 @@
 import jax
 import jax.numpy as jnp
 from jax import lax
+from jax.experimental import pallas as pl
+from jax.experimental.pallas import tpu as pltpu
 from jax.sharding import PartitionSpec as P
 
 TOP = 6
 
 epsilon = 1e-06
+
+LAG_NANOS = 20000
+TURN_LAG_NANOS = 4000
+RETURN_LAG_NANOS = 4000
+AHEAD = 2
+CONTRACT = (((1,), (1,)), ((), ()))
+IN_HBM = pl.BlockSpec(memory_space=pl.ANY)
+IN_SMEM = pl.BlockSpec(memory_space=pltpu.SMEM)
+IN_VMEM = pl.BlockSpec(memory_space=pltpu.VMEM)
+
+
+def late_kernel(nanos_ref, rows_ref, out_ref):
+    pl.delay(nanos_ref[0])
+    out_ref[...] = rows_ref[...]
+
+
+def held_back(rows, nanos):
+    return pl.pallas_call(
+        late_kernel,
+        out_shape=jax.ShapeDtypeStruct(rows.shape, rows.dtype),
+        in_specs=[IN_SMEM, IN_VMEM],
+        out_specs=IN_VMEM,
+        name="held_back",
+    )(nanos.reshape(1), rows)
+
+
+def fetch(pick, own, other, target, sem):
+    def start():
+        @pl.when(pick == 0)
+        def _():
+            pltpu.make_async_copy(own, target, sem).start()
+
+        @pl.when(pick != 0)
+        def _():
+            pltpu.make_async_copy(other, target, sem).start()
+
+        return pltpu.make_async_copy(own, target, sem)
+
+    return start
+
+
+def brought(source, target, sem):
+    return lambda: started(source, target, sem)
+
+
+def started(source, target, sem):
+    copy = pltpu.make_async_copy(source, target, sem)
+    copy.start()
+    return copy
+
+
+def wait_all(copies):
+    for copy in copies:
+        copy.wait()
+
+
+class Incoming:
+    def __init__(self, starters):
+        self.starters = starters
+        self.flying = []
+        self.taken = 0
+        self.launch(1 + AHEAD)
+
+    def launch(self, upto):
+        for start in self.starters[len(self.flying) : upto]:
+            self.flying.append(start())
+
+    def take(self, count):
+        for _ in range(count):
+            self.flying[self.taken].wait()
+            self.taken += 1
+            self.launch(self.taken + 1 + AHEAD)
+
+
+def pieces(total, widths):
+    parts = []
+    at = 0
+    for width in widths:
+        size = min(width, total - at)
+        if size > 0:
+            parts.append(pl.ds(at, size))
+            at += size
+    if at < total:
+        parts.append(pl.ds(at, total - at))
+    return parts
+
+
+def hidden_pieces(total):
+    return pieces(total, (256, 512))
+
+
+def feature_pieces(total):
+    return pieces(total, (1280, 768, 512))
+
+
+def wide_dot(left, right):
+    return jnp.dot(left, right, preferred_element_type=jnp.float32)
+
+
+def turned_dot(left, right):
+    return lax.dot_general(left, right, CONTRACT, preferred_element_type=jnp.float32)
+
+
+def gate_grads(d_act, gate_pre, up_val):
+    sigmoid_g = jax.nn.sigmoid(gate_pre)
+    d_gate = d_act * up_val * sigmoid_g * (1.0 + gate_pre * (1.0 - sigmoid_g))
+    d_up = d_act * gate_pre * sigmoid_g
+    return d_gate.astype(jnp.bfloat16), d_up.astype(jnp.bfloat16)
+
+
+def forward_kernel(
+    pick_ref, rows_hbm, gate_a, up_a, down_a, gate_b, up_b, down_b,
+    out_hbm, pre_hbm, val_hbm,
+    rows, gate, up, down, pre, val, act, out, in_sem, gate_sem, up_sem, down_sem, pre_sem, val_sem, out_sem,
+):
+    pick = pick_ref[0]
+    hidden_parts = hidden_pieces(gate.shape[1])
+    feature_parts = feature_pieces(down.shape[1])
+    line = [brought(rows_hbm, rows, in_sem)]
+    for n, part in enumerate(hidden_parts):
+        line.append(fetch(pick, gate_a.at[:, part], gate_b.at[:, part], gate.at[:, part], gate_sem.at[n]))
+        line.append(fetch(pick, up_a.at[:, part], up_b.at[:, part], up.at[:, part], up_sem.at[n]))
+    for n, part in enumerate(feature_parts):
+        line.append(fetch(pick, down_a.at[:, part], down_b.at[:, part], down.at[:, part], down_sem.at[n]))
+    incoming = Incoming(line)
+    incoming.take(1)
+    leaving = []
+    for n, part in enumerate(hidden_parts):
+        incoming.take(1)
+        gate_pre = wide_dot(rows[...], gate[:, part])
+        pre[:, part] = gate_pre
+        incoming.take(1)
+        up_val = wide_dot(rows[...], up[:, part])
+        val[:, part] = up_val
+        act[:, part] = (gate_pre * jax.nn.sigmoid(gate_pre) * up_val).astype(jnp.bfloat16)
+        leaving.append(started(pre.at[:, part], pre_hbm.at[:, part], pre_sem.at[n]))
+        leaving.append(started(val.at[:, part], val_hbm.at[:, part], val_sem.at[n]))
+    for n, part in enumerate(feature_parts):
+        incoming.take(1)
+        out[:, part] = wide_dot(act[...], down[:, part]).astype(jnp.bfloat16)
+        leaving.append(started(out.at[:, part], out_hbm.at[:, part], out_sem.at[n]))
+    wait_all(leaving)
+
+
+def expert_forward(pick, rows, own, other):
+    slots, feat = rows.shape
+    hidden = own[0].shape[1]
+    count = len(hidden_pieces(hidden))
+    wide = len(feature_pieces(feat))
+    bf16, f32 = jnp.bfloat16, jnp.float32
+    return pl.pallas_call(
+        forward_kernel,
+        out_shape=(
+            jax.ShapeDtypeStruct((slots, feat), bf16),
+            jax.ShapeDtypeStruct((slots, hidden), f32),
+            jax.ShapeDtypeStruct((slots, hidden), f32),
+        ),
+        in_specs=[IN_SMEM] + [IN_HBM] * 7,
+        out_specs=(IN_HBM,) * 3,
+        scratch_shapes=[
+            pltpu.VMEM((slots, feat), bf16),
+            pltpu.VMEM((feat, hidden), bf16),
+            pltpu.VMEM((feat, hidden), bf16),
+            pltpu.VMEM((hidden, feat), bf16),
+            pltpu.VMEM((slots, hidden), f32),
+            pltpu.VMEM((slots, hidden), f32),
+            pltpu.VMEM((slots, hidden), bf16),
+            pltpu.VMEM((slots, feat), bf16),
+            pltpu.SemaphoreType.DMA(()),
+            pltpu.SemaphoreType.DMA((count,)),
+            pltpu.SemaphoreType.DMA((count,)),
+            pltpu.SemaphoreType.DMA((wide,)),
+            pltpu.SemaphoreType.DMA((count,)),
+            pltpu.SemaphoreType.DMA((count,)),
+            pltpu.SemaphoreType.DMA((wide,)),
+        ],
+        name="expert_forward",
+    )(pick.reshape(1), rows, *own, *other)
+
+
+def backward_kernel(
+    pick_ref, rows_hbm, pre_hbm, val_hbm, gate_a, up_a, down_a, gate_b, up_b, down_b,
+    out_hbm,
+    rows, gate, up, down, pre, val, d_gate, d_up, out, in_sem, gate_sem, up_sem, down_sem, pre_sem, val_sem, out_sem,
+):
+    pick = pick_ref[0]
+    hidden_parts = hidden_pieces(gate.shape[1])
+    feature_parts = feature_pieces(down.shape[1])
+    line = [brought(rows_hbm, rows, in_sem)]
+    for n, part in enumerate(hidden_parts):
+        line.append(fetch(pick, down_a.at[part, :], down_b.at[part, :], down.at[part, :], down_sem.at[n]))
+        line.append(brought(pre_hbm.at[:, part], pre.at[:, part], pre_sem.at[n]))
+        line.append(brought(val_hbm.at[:, part], val.at[:, part], val_sem.at[n]))
+    for n, part in enumerate(feature_parts):
+        line.append(fetch(pick, gate_a.at[part, :], gate_b.at[part, :], gate.at[part, :], gate_sem.at[n]))
+        line.append(fetch(pick, up_a.at[part, :], up_b.at[part, :], up.at[part, :], up_sem.at[n]))
+    incoming = Incoming(line)
+    incoming.take(1)
+    for part in hidden_parts:
+        incoming.take(1)
+        d_act = turned_dot(rows[...], down[part, :])
+        incoming.take(2)
+        part_gate, part_up = gate_grads(d_act, pre[:, part], val[:, part])
+        d_gate[:, part] = part_gate
+        d_up[:, part] = part_up
+    leaving = []
+    for n, part in enumerate(feature_parts):
+        incoming.take(2)
+        summed = turned_dot(d_gate[...], gate[part, :]) + turned_dot(d_up[...], up[part, :])
+        out[:, part] = summed.astype(jnp.bfloat16)
+        leaving.append(started(out.at[:, part], out_hbm.at[:, part], out_sem.at[n]))
+    wait_all(leaving)
+
+
+def expert_backward(pick, rows, pre, val, own, other):
+    slots, feat = rows.shape
+    hidden = own[0].shape[1]
+    count = len(hidden_pieces(hidden))
+    wide = len(feature_pieces(feat))
+    bf16, f32 = jnp.bfloat16, jnp.float32
+    return pl.pallas_call(
+        backward_kernel,
+        out_shape=jax.ShapeDtypeStruct((slots, feat), bf16),
+        in_specs=[IN_SMEM] + [IN_HBM] * 9,
+        out_specs=IN_HBM,
+        scratch_shapes=[
+            pltpu.VMEM((slots, feat), bf16),
+            pltpu.VMEM((feat, hidden), bf16),
+            pltpu.VMEM((feat, hidden), bf16),
+            pltpu.VMEM((hidden, feat), bf16),
+            pltpu.VMEM((slots, hidden), f32),
+            pltpu.VMEM((slots, hidden), f32),
+            pltpu.VMEM((slots, hidden), bf16),
+            pltpu.VMEM((slots, hidden), bf16),
+            pltpu.VMEM((slots, feat), bf16),
+            pltpu.SemaphoreType.DMA(()),
+            pltpu.SemaphoreType.DMA((wide,)),
+            pltpu.SemaphoreType.DMA((wide,)),
+            pltpu.SemaphoreType.DMA((count,)),
+            pltpu.SemaphoreType.DMA((count,)),
+            pltpu.SemaphoreType.DMA((count,)),
+            pltpu.SemaphoreType.DMA((wide,)),
+        ],
+        name="expert_backward",
+    )(pick.reshape(1), rows, pre, val, *own, *other)
+
+
+def joint_kernel(
+    pick_ref, rows_hbm, d_act_hbm, gate_a, up_a, gate_b, up_b,
+    act_hbm, out_hbm,
+    rows, gate, up, d_act, act, d_gate, d_up, out, in_sem, gate_sem, up_sem, d_act_sem, act_sem, out_sem,
+):
+    pick = pick_ref[0]
+    hidden_parts = hidden_pieces(gate.shape[1])
+    feature_parts = feature_pieces(out.shape[1])
+    line = [brought(rows_hbm, rows, in_sem)]
+    for n, part in enumerate(hidden_parts):
+        line.append(fetch(pick, gate_a.at[:, part], gate_b.at[:, part], gate.at[:, part], gate_sem.at[n]))
+        line.append(fetch(pick, up_a.at[:, part], up_b.at[:, part], up.at[:, part], up_sem.at[n]))
+        line.append(brought(d_act_hbm.at[:, part], d_act.at[:, part], d_act_sem.at[n]))
+    incoming = Incoming(line)
+    incoming.take(1)
+    leaving = []
+    for n, part in enumerate(hidden_parts):
+        incoming.take(1)
+        gate_pre = wide_dot(rows[...], gate[:, part])
+        incoming.take(1)
+        up_val = wide_dot(rows[...], up[:, part])
+        act[:, part] = (gate_pre * jax.nn.sigmoid(gate_pre) * up_val).astype(jnp.bfloat16)
+        leaving.append(started(act.at[:, part], act_hbm.at[:, part], act_sem.at[n]))
+        incoming.take(1)
+        part_gate, part_up = gate_grads(d_act[:, part], gate_pre, up_val)
+        d_gate[:, part] = part_gate
+        d_up[:, part] = part_up
+    for n, part in enumerate(feature_parts):
+        summed = turned_dot(d_gate[...], gate[part, :]) + turned_dot(d_up[...], up[part, :])
+        out[:, part] = summed.astype(jnp.bfloat16)
+        leaving.append(started(out.at[:, part], out_hbm.at[:, part], out_sem.at[n]))
+    wait_all(leaving)
+
+
+def expert_joint(pick, rows, d_act, own, other):
+    slots, feat = rows.shape
+    hidden = own[0].shape[1]
+    count = len(hidden_pieces(hidden))
+    wide = len(feature_pieces(feat))
+    bf16, f32 = jnp.bfloat16, jnp.float32
+    return pl.pallas_call(
+        joint_kernel,
+        out_shape=(
+            jax.ShapeDtypeStruct((slots, hidden), bf16),
+            jax.ShapeDtypeStruct((slots, feat), bf16),
+        ),
+        in_specs=[IN_SMEM] + [IN_HBM] * 6,
+        out_specs=(IN_HBM,) * 2,
+        scratch_shapes=[
+            pltpu.VMEM((slots, feat), bf16),
+            pltpu.VMEM((feat, hidden), bf16),
+            pltpu.VMEM((feat, hidden), bf16),
+            pltpu.VMEM((slots, hidden), f32),
+            pltpu.VMEM((slots, hidden), bf16),
+            pltpu.VMEM((slots, hidden), bf16),
+            pltpu.VMEM((slots, hidden), bf16),
+            pltpu.VMEM((slots, feat), bf16),
+            pltpu.SemaphoreType.DMA(()),
+            pltpu.SemaphoreType.DMA((count,)),
+            pltpu.SemaphoreType.DMA((count,)),
+            pltpu.SemaphoreType.DMA((count,)),
+            pltpu.SemaphoreType.DMA((count,)),
+            pltpu.SemaphoreType.DMA((wide,)),
+        ],
+        name="expert_joint",
+    )(pick.reshape(1), rows, d_act, *own[:2], *other[:2])
 
 
 def exchange(rows):
@@ -57,33 +372,12 @@
     return (wide_in * inverse_rms(wide_in) * gain).astype(jnp.bfloat16)
 
 
-def hidden_forward(rows, gate_mat, up_mat):
-    gate_pre = jnp.dot(rows, gate_mat, preferred_element_type=jnp.float32)
-    up_val = jnp.dot(rows, up_mat, preferred_element_type=jnp.float32)
-    activated = (jax.nn.silu(gate_pre) * up_val).astype(jnp.bfloat16)
-    return activated, gate_pre, up_val
-
-
 def project_down(activated, down_mat):
     return jnp.dot(activated, down_mat, preferred_element_type=jnp.float32).astype(jnp.bfloat16)
 
 
-CONTRACT = (((1,), (1,)), ((), ()))
-
-
 def hidden_grad(d_rows, down_mat):
     return lax.dot_general(d_rows, down_mat, CONTRACT, preferred_element_type=jnp.float32)
-
-
-def rows_grad(d_act, gate_pre, up_val, gate_mat, up_mat):
-    sigmoid_g = jax.nn.sigmoid(gate_pre)
-    d_gate = (d_act * up_val * sigmoid_g * (1.0 + gate_pre * (1.0 - sigmoid_g))).astype(
-        jnp.bfloat16
-    )
-    d_up = (d_act * gate_pre * sigmoid_g).astype(jnp.bfloat16)
-    summed = lax.dot_general(d_gate, gate_mat, CONTRACT, preferred_element_type=jnp.float32)
-    summed = summed + lax.dot_general(d_up, up_mat, CONTRACT, preferred_element_type=jnp.float32)
-    return summed.astype(jnp.bfloat16)
 
 
 def layer_grad(dy, layer_in, gain, picks, returned):
@@ -138,6 +432,9 @@
             values,
         )
 
+    low_pick = mine.astype(jnp.int32)
+    high_pick = 1 - low_pick
+
     picks_low, mix_low = slot_matrices(route_low, gate_low, experts, capacity)
     picks_high, mix_high = slot_matrices(route_high, gate_high, experts, capacity)
     scale_low = jnp.sum(mix_low, axis=0)[:, None]
@@ -146,6 +443,7 @@
     first_in = of_micro(inputs, mine)
     last_grad = of_micro(cotangent, mine)
     source = jnp.where(early, normed_rows(first_in, gain_low), last_grad)
+    source = held_back(source, jnp.where(mine == 1, LAG_NANOS, 0).astype(jnp.int32))
     picks_first = jnp.where(early, picks_low, picks_high)
     scale_first = jnp.where(early, 1.0, scale_high)
     arrived = exchange((scale_first * spread(picks_first, source)).astype(jnp.bfloat16))
@@ -156,30 +454,17 @@
     def send_grads(dy, picks, scale):
         return exchange((scale * spread(picks, dy)).astype(jnp.bfloat16))
 
-    def run_forward(held, mats):
-        activated, gate_pre, up_val = hidden_forward(held[0], mats[0], mats[1])
-        return project_down(activated, mats[2]), gate_pre, up_val
-
     def mixed(layer_in, mix, returned):
         return (layer_in.astype(jnp.float32) + gathered_sum(mix, returned)).astype(jnp.bfloat16)
 
-    def run_backward(held, mats):
-        d_rows, gate_pre, up_val = held
-        return rows_grad(hidden_grad(d_rows, mats[2]), gate_pre, up_val, mats[0], mats[1])
-
-    def run_joint(held, mats):
-        rows, d_act = held
-        activated, gate_pre, up_val = hidden_forward(rows, mats[0], mats[1])
-        return activated, rows_grad(d_act, gate_pre, up_val, mats[0], mats[1])
-
     no_rows = jnp.zeros((tok_rows, feat_width), jnp.bfloat16)
     no_hidden = jnp.zeros((slots, hidden), jnp.float32)
 
     def climb(got):
-        out_low, pre_low, up_low = with_mats(0, run_forward, got)
+        out_low, pre_low, up_low = expert_forward(low_pick, got, own_mats, other_mats)
         state_low = mixed(first_in, mix_low, exchange(out_low))
         got_high = send_rows(state_low, gain_high, picks_high)
-        out_high, pre_high, up_high = with_mats(1, run_forward, got_high)
+        out_high, pre_high, up_high = expert_forward(high_pick, got_high, own_mats, other_mats)
         state_high = mixed(state_low, mix_high, exchange(out_high))
         return state_low, state_high, pre_low, up_low, pre_high, up_high
 
@@ -192,16 +477,18 @@
     )
     relayed = lax.ppermute(state_high, "segment", [(0, 2), (1, 3)])
 
+    relayed = held_back(relayed, jnp.where(mine == 1, TURN_LAG_NANOS, 0).astype(jnp.int32))
+
     def turn(held):
         layer_in, d_act = held
         got_low = send_rows(layer_in, gain_low, picks_low)
-        out_low, pre_low, up_low = with_mats(0, run_forward, got_low)
+        out_low, pre_low, up_low = expert_forward(low_pick, got_low, own_mats, other_mats)
         state = mixed(layer_in, mix_low, exchange(out_low))
         got_high = send_rows(state, gain_high, picks_high)
-        activated, d_rows = with_mats(1, run_joint, got_high, d_act)
+        activated, d_rows = expert_joint(high_pick, got_high, d_act, own_mats, other_mats)
         grad_high = layer_grad(last_grad, state, gain_high, picks_high, exchange(d_rows))
         d_got = send_grads(grad_high, picks_low, scale_low)
-        d_rows_low = with_mats(0, run_backward, d_got, pre_low, up_low)
+        d_rows_low = expert_backward(low_pick, d_got, pre_low, up_low, own_mats, other_mats)
         grad_low = layer_grad(grad_high, layer_in, gain_low, picks_low, exchange(d_rows_low))
         return state, activated, grad_high, grad_low
 
@@ -211,12 +498,14 @@
     turn_state, activated, turn_high, turn_low = lax.cond(early, stay, turn, (relayed, kept_a))
     came_back = lax.ppermute(turn_low, "segment", [(2, 0), (3, 1)])
 
+    came_back = held_back(came_back, jnp.where(mine == 1, RETURN_LAG_NANOS, 0).astype(jnp.int32))
+
     def descend(dy):
         d_got = send_grads(dy, picks_high, scale_high)
-        d_rows_high = with_mats(1, run_backward, d_got, kept_c, kept_d)
+        d_rows_high = expert_backward(high_pick, d_got, kept_c, kept_d, own_mats, other_mats)
         grad_high = layer_grad(dy, state_low, gain_high, picks_high, exchange(d_rows_high))
         d_got_low = send_grads(grad_high, picks_low, scale_low)
-        d_rows_low = with_mats(0, run_backward, d_got_low, kept_a, kept_b)
+        d_rows_low = expert_backward(low_pick, d_got_low, kept_a, kept_b, own_mats, other_mats)
         grad_low = layer_grad(grad_high, first_in, gain_low, picks_low, exchange(d_rows_low))
         return state_low, state_high, grad_low, grad_high
 

time: 804 us -> 611 us (0.76)
  waiting for transfers between devices: 582 us -> 345 us
  Pallas kernels: 0 us -> 87.9 us
  blocking collectives: 0 us -> 86.1 us
  matrix products: 82.7 us -> 12.4 us
  starting transfers between devices: 77.9 us -> 34.1 us
  loops' own time: 20.4 us -> 9.24 us
  other arithmetic: 25.9 us -> 16 us
    all_to_all x8 -> x5, waiting for transfers between devices: 256 us -> 112 us  [exchange(): lax.all_to_all(blocks, 'expert', split_axis=0, concat_axis=0, tiled=True)]
    ppermute x1, waiting for transfers between devices: 319 us -> 227 us  [local(): came_back = lax.ppermute(turn_low, 'segment', [(2, 0), (3, 1)])]
    pallas_call x0 -> x7, Pallas kernels: none -> 87.9 us  [the longest x2 32.2 us: expert_backward(): pl.pallas_call(backward_kernel, out_shape=jax.ShapeDtypeStruct((slots, fe...]
    all_to_all x0 -> x3, blocking collectives: none -> 86.1 us  [exchange(): lax.all_to_all(blocks, 'expert', split_axis=0, concat_axis=0, tiled=True)]
    dot_general x12 -> x0, matrix products: 66.7 us -> none  [the longest x2 15.1 us: rows_grad(): lax.dot_general(d_gate, gate_mat, CONTRACT, preferred_element_type=jnp.fl...]
    all_to_all x8 -> x5, starting transfers between devices: 72.3 us -> 28.7 us  [exchange(): lax.all_to_all(blocks, 'expert', split_axis=0, concat_axis=0, tiled=True)]
    unnamed x4 -> x0, loops' own time: 12.6 us -> none
    convert_element_type x2 -> x0, other arithmetic: 12.5 us -> none  [rows_grad(): return summed.astype(jnp.bfloat16)]
  transfers between devices with their start and end apart: 17 -> 14, of which waited for: 11 -> 8; matrix products, arithmetic and copies ran while one was open for 1% -> 2% of each run, Pallas kernels for 0% -> 4%
where the time goes in v2:
time: 611 us; the launch traced here: 601 us
  waiting for transfers between devices  345 us (56%)
  Pallas kernels  87.9 us (14%)
  blocking collectives  86.1 us (14%)
  starting transfers between devices  34.1 us (6%)
  other arithmetic  16 us (3%)
  matrix products  12.4 us (2%)
  loops' own time  9.24 us (2%)
  local copies, waits for them, and re-layouts  8.82 us (1%)
    ppermute x1, waiting for transfers between devices, local(): came_back = lax.ppermute(turn_low, 'segment', [(2, 0), (3, 1)])  227 us
    all_to_all x5, waiting for transfers between devices, exchange(): lax.all_to_all(blocks, 'expert', split_axis=0, concat_axis=0, tiled=True)  112 us
    all_to_all x3, blocking collectives, exchange(): lax.all_to_all(blocks, 'expert', split_axis=0, concat_axis=0, tiled=True)  86.1 us
    pallas_call x2, Pallas kernels, expert_backward(): pl.pallas_call(backward_kernel, out_shape=jax.ShapeDtypeStruct((slots, fe...  32.2 us
    pallas_call x3, Pallas kernels, held_back(): pl.pallas_call(late_kernel, out_shape=jax.ShapeDtypeStruct(rows.shape, ro...  31.7 us
    all_to_all x5, starting transfers between devices, exchange(): lax.all_to_all(blocks, 'expert', split_axis=0, concat_axis=0, tiled=True)  28.7 us
    pallas_call x2, Pallas kernels, expert_forward(): pl.pallas_call(forward_kernel, out_shape=(jax.ShapeDtypeStruct((slots, fe...  23.9 us
  transfers between devices with their start and end apart: 14, of which 8 were waited for; matrix products, arithmetic and copies ran while one was open for 2% of the time, Pallas kernels for 4%

profile of v2, /device:TPU:1, one launch (start us, length us, event | category | flops | bytes accessed | tf_op | source)
XLA Modules:
  0.0 601.0 jit_solution(6714435544188060029)
XLA Ops:
  1.4 1.5 collective-permute-start.1
  4.8 1.1 fusion.73
  7.5 1.1 select_reduce_fusion
  9.2 1.3 fusion.87
  10.5 2.0 fusion.76
  12.5 21.7 %held_back.3 = bf16[64,2560]{1,0:T(8,128)(2,1)} custom-call(s32[1]{0:T(128)} %bitcast.52.nanos_ref, bf16[64,2560]{1,0:T(8,128)(2,1)} %get-tuple-element.284.rows_ref), custom_call_target="tpu_custom_call" | custom-call | tf_op jit(solution)/shard_map/held_back/pallas_call | solution.py:28
  34.2 3.4 multiply_convert_fusion.3
  37.6 10.6 %all-to-all-start.14 = ((bf16[32,16,2560]{2,1,0:T(8,128)(2,1)}), bf16[32,16,2560]{2,1,0:T(8,128)(2,1)S(1)}, u32[]{:S(2)}, u32[]{:S(2)}) async-start(bf16[32,16,2560]{2,1,0:T(8,128)(2,1)} %bitcast.55), calls=%async_computation.14 | async-start | bytes 5242880 | tf_op jit(solution)/shard_map/all_to_all | solution.py:330
  48.3 21.3 %all-to-all-done.14 = bf16[32,16,2560]{2,1,0:T(8,128)(2,1)S(1)} async-done(((bf16[32,16,2560]{2,1,0:T(8,128)(2,1)}), bf16[32,16,2560]{2,1,0:T(8,128)(2,1)S(1)}, u32[]{:S(2)}, u32[]{:S(2)}) %all-to-all-start.14) | async-done | bytes 2621472 | tf_op jit(solution)/shard_map/all_to_all | solution.py:330
  69.6 116.6 %conditional.9 = (bf16[64,2560]{1,0:T(8,128)(2,1)}, bf16[64,2560]{1,0:T(8,128)(2,1)S(1)}, f32[512,768]{1,0:T(8,128)}, f32[512,768]{1,0:T(8,128)}, f32[512,768]{1,0:T(8,128)}, /*index=5*/f32[512,768]{1,0:T(8,128)}) conditional(s32[]{:T(128)} %convert_element_type.164, (s32[]{:T(128)}, bf16[512,2560]{1,0:T(8,128)(2,1)S(1)}, ...), branch_computations={%region_8.11_spmd, %region_11.13_spmd} | conditional | flops 2013265920 | bytes 37125264 | solution.py:475
  69.6 11.4 %expert_forward.3 = (bf16[512,2560]{1,0:T(8,128)(2,1)}, f32[512,768]{1,0:T(8,128)}, f32[512,768]{1,0:T(8,128)}) custom-call(s32[1]{0:T(128)} %bitcast.pick_ref, bf16[512,2560]{1,0:T(8,128)(2,1)S(1)} %get-tuple-element.167.rows_hbm, bf16[2560,768]{1,0:T(8,128)(2,1)} %get-tuple-element.168.gate_a, bf16[2560,768]{1,0:T(8,128)(2,1)} %get-tuple-element.169.up_a, ...), custom_call_target="tpu_custom_call" | custom-call | tf_op jit(solution)/shard_map/cond/branch_1_fun/expert_forward/pallas_call | solution.py:161
  81.1 5.5 all-to-all-start
  86.6 22.0 %all-to-all-done = bf16[32,16,2560]{2,1,0:T(8,128)(2,1)S(1)} async-done(((bf16[32,16,2560]{2,1,0:T(8,128)(2,1)}), bf16[32,16,2560]{2,1,0:T(8,128)(2,1)S(1)}, u32[]{:S(2)}, u32[]{:S(2)}) %all-to-all-start) | async-done | bytes 2621472 | tf_op jit(solution)/shard_map/cond/branch_1_fun/all_to_all | solution.py:330
  109.1 0.9 fusion.9
  110.1 1.9 convolution_convert_fusion
  111.9 31.7 %all_to_all.61 = bf16[32,16,2560]{2,1,0:T(8,128)(2,1)} all-to-all(bf16[32,16,2560]{2,1,0:T(8,128)(2,1)S(1)} %bitcast.156), channel_id=1, replica_groups=mesh['segment'=4,'expert'=32] {'expert'}, dimensions={0} | all-to-all | bytes 5242880 | tf_op jit(solution)/shard_map/cond/branch_1_fun/all_to_all | solution.py:330
  143.7 12.5 %expert_forward.4 = (bf16[512,2560]{1,0:T(8,128)(2,1)}, f32[512,768]{1,0:T(8,128)}, f32[512,768]{1,0:T(8,128)}) custom-call(s32[1]{0:T(128)} %bitcast.3.pick_ref, bf16[512,2560]{1,0:T(8,128)(2,1)} %bitcast.164, bf16[2560,768]{1,0:T(8,128)(2,1)} %get-tuple-element.168.gate_a, bf16[2560,768]{1,0:T(8,128)(2,1)} %get-tuple-element.169.up_a, ...), custom_call_target="tpu_custom_call" | custom-call | tf_op jit(solution)/shard_map/cond/branch_1_fun/expert_forward/pallas_call | solution.py:161
  156.2 4.1 all-to-all-start.2
  160.3 23.9 %all-to-all-done.2 = bf16[32,16,2560]{2,1,0:T(8,128)(2,1)S(1)} async-done(((bf16[32,16,2560]{2,1,0:T(8,128)(2,1)}), bf16[32,16,2560]{2,1,0:T(8,128)(2,1)S(1)}, u32[]{:S(2)}, u32[]{:S(2)}) %all-to-all-start.2) | async-done | bytes 2621472 | tf_op jit(solution)/shard_map/cond/branch_1_fun/all_to_all | solution.py:330
  184.8 1.1 fusion.12
  186.2 1.3 collective-permute-start.6
  187.6 4.0 collective-permute-done.6.rows_ref
  192.2 5.0 held_back.4
  197.3 9.9 %conditional.10 = (bf16[64,2560]{1,0:T(8,128)(2,1)S(1)}, bf16[512,768]{1,0:T(8,128)(2,1)S(1)}, bf16[64,2560]{1,0:T(8,128)(2,1)}, bf16[64,2560]{1,0:T(8,128)(2,1)}) conditional(s32[]{:T(128)} %convert_element_type.164, (bf16[64,2560]{1,0:T(8,128)(2,1)S(1)}, f32[64,512]{1,0:T(8,128)}, s32[]{:T(128)}, f32[1,2560]{1,0:T(1,128)}, ...), branch_computations={%region_14.19_spmd, %region_19.20_spmd} | conditional | flops 1186922752 | bytes 62450500 | solution.py:498
  207.2 1.3 collective-permute-start.7
  208.5 227.2 %collective-permute-done.7.rows_ref = bf16[64,2560]{1,0:T(8,128)(2,1)S(1)} collective-permute-done((bf16[64,2560]{1,0:T(8,128)(2,1)}, bf16[64,2560]{1,0:T(8,128)(2,1)S(1)}, u32[]{:S(2)}, u32[]{:S(2)}) %collective-permute-start.7) | collective-permute-done | bytes 327712 | tf_op jit(solution)/shard_map/ppermute | solution.py:499
  436.4 5.0 held_back.5
  441.4 152.4 %conditional.11 = (bf16[64,2560]{1,0:T(8,128)(2,1)S(1)}, bf16[64,2560]{1,0:T(8,128)(2,1)}, bf16[64,2560]{1,0:T(8,128)(2,1)}, bf16[1,64,2560]{2,1,0:T(8,128)(2,1)}) conditional(s32[]{:T(128)} %convert_element_type.164, (bf16[64,2560]{1,0:T(8,128)(2,1)S(1)}, f32[64,512]{1,0:T(8,128)S(1)}, s32[]{:T(128)}, bf16[512,768]{1,0:T(8,128)(2,1)S(1)}, ...), branch_computations={%region_20.23_spmd, %region_23.28_spmd} | conditional | flops 2349858816 | bytes 45593760 | solution.py:517
  441.4 1.5 multiply_convert_fusion.2
  442.9 25.5 %all_to_all.67 = bf16[32,16,2560]{2,1,0:T(8,128)(2,1)} all-to-all(bf16[32,16,2560]{2,1,0:T(8,128)(2,1)S(1)} %bitcast.160), channel_id=1, replica_groups=mesh['segment'=4,'expert'=32] {'expert'}, dimensions={0} | all-to-all | bytes 5242880 | tf_op jit(solution)/shard_map/cond/branch_1_fun/all_to_all | solution.py:330
  468.4 16.2 %expert_backward.4 = bf16[512,2560]{1,0:T(8,128)(2,1)} custom-call(s32[1]{0:T(128)} %bitcast.32.pick_ref, bf16[512,2560]{1,0:T(8,128)(2,1)} %bitcast.146, f32[512,768]{1,0:T(8,128)} %get-tuple-element.224.pre_hbm, f32[512,768]{1,0:T(8,128)} %get-tuple-element.225.val_hbm, bf16[2560,768]{1,0:T(8,128)(2,1)} %get-tuple-element.226.gate_a, ...), custom_call_target="tpu_custom_call" | custom-call | tf_op jit(solution)/shard_map/cond/branch_1_fun/expert_backward/pallas_call | solution.py:231
  484.6 4.3 all-to-all-start.11
  488.9 26.0 %all-to-all-done.11 = bf16[32,16,2560]{2,1,0:T(8,128)(2,1)S(1)} async-done(((bf16[32,16,2560]{2,1,0:T(8,128)(2,1)}), bf16[32,16,2560]{2,1,0:T(8,128)(2,1)S(1)}, u32[]{:S(2)}, u32[]{:S(2)}) %all-to-all-start.11) | async-done | bytes 2621472 | tf_op jit(solution)/shard_map/cond/branch_1_fun/all_to_all | solution.py:330
  514.9 1.6 fusion.61
  516.6 2.0 fusion.64
  518.6 1.9 multiply_convert_fusion.1
  520.4 28.9 %all_to_all.68 = bf16[32,16,2560]{2,1,0:T(8,128)(2,1)} all-to-all(bf16[32,16,2560]{2,1,0:T(8,128)(2,1)S(1)} %bitcast.161), channel_id=1, replica_groups=mesh['segment'=4,'expert'=32] {'expert'}, dimensions={0} | all-to-all | bytes 5242880 | tf_op jit(solution)/shard_map/cond/branch_1_fun/all_to_all | solution.py:330
  549.4 16.1 %expert_backward.5 = bf16[512,2560]{1,0:T(8,128)(2,1)} custom-call(s32[1]{0:T(128)} %bitcast.38.pick_ref, bf16[512,2560]{1,0:T(8,128)(2,1)} %bitcast.147, f32[512,768]{1,0:T(8,128)} %get-tuple-element.237.pre_hbm, f32[512,768]{1,0:T(8,128)} %get-tuple-element.238.val_hbm, bf16[2560,768]{1,0:T(8,128)(2,1)} %get-tuple-element.226.gate_a, ...), custom_call_target="tpu_custom_call" | custom-call | tf_op jit(solution)/shard_map/cond/branch_1_fun/expert_backward/pallas_call | solution.py:231
  565.4 4.2 all-to-all-start.13
  569.6 1.0 copy.82
  570.7 1.7 copy.85
  572.4 18.5 %all-to-all-done.13 = bf16[32,16,2560]{2,1,0:T(8,128)(2,1)S(1)} async-done(((bf16[32,16,2560]{2,1,0:T(8,128)(2,1)}), bf16[32,16,2560]{2,1,0:T(8,128)(2,1)S(1)}, u32[]{:S(2)}, u32[]{:S(2)}) %all-to-all-start.13) | async-done | bytes 2621472 | tf_op jit(solution)/shard_map/cond/branch_1_fun/all_to_all | solution.py:330
  591.6 2.0 fusion.69
  593.9 1.3 broadcast_select_fusion.2
  595.2 2.1 collective-permute-done.8
  597.3 1.3 broadcast_select_fusion.1
  598.7 0.9 maximum_bitcast_fusion.1
  599.6 0.9 maximum_bitcast_fusion
  (68 shorter events, 9.8 us)
Async XLA Ops:
  1.4 6.1 %collective-permute-start.1 = (f32[64,6]{0,1:T(8,128)S(1)}, f32[64,6]{0,1:T(8,128)S(1)}, u32[]{:S(2)}, u32[]{:S(2)}) collective-permute-start(f32[64,6]{0,1:T(8,128)S(1)} %bitcast.177), channel_id=1, source_target_pairs={{0,32},{32,0},{64,96},{96,64},{1,33},{33,1},{65,97},{97,65},{2,34}... | collective-permute-start | bytes 4616 | tf_op jit(solution)/shard_map/ppermute | solution.py:407
  3.7 2.3 collective-permute-start
  3.8 5.4 collective-permute-start.2
  4.3 65.3 %collective-permute-start.4 = (bf16[2560,768]{1,0:T(8,128)(2,1)}, bf16[2560,768]{1,0:T(8,128)(2,1)}, u32[]{:S(2)}, u32[]{:S(2)}) collective-permute-start(bf16[2560,768]{1,0:T(8,128)(2,1)} %bitcast.126), channel_id=1, source_target_pairs={{0,32},{32,0},{64,96},{96,64},{1,33},{33,1},{65,97},{97,65},{2,34}... | collective-permute-start | bytes 11796488 | tf_op jit(solution)/shard_map/ppermute | solution.py:407
  4.4 65.2 %collective-permute-start.5 = (bf16[2560,768]{1,0:T(8,128)(2,1)}, bf16[2560,768]{1,0:T(8,128)(2,1)}, u32[]{:S(2)}, u32[]{:S(2)}) collective-permute-start(bf16[2560,768]{1,0:T(8,128)(2,1)} %bitcast.130), channel_id=1, source_target_pairs={{0,32},{32,0},{64,96},{96,64},{1,33},{33,1},{65,97},{97,65},{2,34}... | collective-permute-start | bytes 11796488 | tf_op jit(solution)/shard_map/ppermute | solution.py:407
  5.9 63.7 %copy-start = (bf16[64,2560]{1,0:T(8,128)(2,1)}, bf16[64,2560]{1,0:T(8,128)(2,1)S(1)}, u32[]{:S(2)}) copy-start(bf16[64,2560]{1,0:T(8,128)(2,1)S(1)} %get-tuple-element.287) | copy-start | bytes 983044
  6.0 63.6 %collective-permute-start.3 = (bf16[768,2560]{1,0:T(8,128)(2,1)}, bf16[768,2560]{1,0:T(8,128)(2,1)}, u32[]{:S(2)}, u32[]{:S(2)}) collective-permute-start(bf16[768,2560]{1,0:T(8,128)(2,1)} %bitcast.134), channel_id=1, source_target_pairs={{0,32},{32,0},{64,96},{96,64},{1,33},{33,1},{65,97},{97,65},{2,34}... | collective-permute-start | bytes 11796488 | tf_op jit(solution)/shard_map/ppermute | solution.py:407
  8.6 0.5 copy-start.14
  37.6 31.9 %all-to-all-start.14 = ((bf16[32,16,2560]{2,1,0:T(8,128)(2,1)}), bf16[32,16,2560]{2,1,0:T(8,128)(2,1)S(1)}, u32[]{:S(2)}, u32[]{:S(2)}) async-start(bf16[32,16,2560]{2,1,0:T(8,128)(2,1)} %bitcast.55), calls=%async_computation.14 | async-start | bytes 5242880 | tf_op jit(solution)/shard_map/all_to_all | solution.py:330
  81.0 5.5 copy-start.5
  81.1 27.5 %all-to-all-start = ((bf16[32,16,2560]{2,1,0:T(8,128)(2,1)}), bf16[32,16,2560]{2,1,0:T(8,128)(2,1)S(1)}, u32[]{:S(2)}, u32[]{:S(2)}) async-start(bf16[32,16,2560]{2,1,0:T(8,128)(2,1)} %bitcast.168), calls=%async_computation | async-start | bytes 5242880 | tf_op jit(solution)/shard_map/cond/branch_1_fun/all_to_all | solution.py:330
  156.2 28.0 %all-to-all-start.2 = ((bf16[32,16,2560]{2,1,0:T(8,128)(2,1)}), bf16[32,16,2560]{2,1,0:T(8,128)(2,1)S(1)}, u32[]{:S(2)}, u32[]{:S(2)}) async-start(bf16[32,16,2560]{2,1,0:T(8,128)(2,1)} %bitcast.169), calls=%async_computation.2 | async-start | bytes 5242880 | tf_op jit(solution)/shard_map/cond/branch_1_fun/all_to_all | solution.py:330
  186.2 11.0 %copy-start.3 = (bf16[64,2560]{1,0:T(8,128)(2,1)}, bf16[64,2560]{1,0:T(8,128)(2,1)S(1)}, u32[]{:S(2)}) copy-start(bf16[64,2560]{1,0:T(8,128)(2,1)S(1)} %get-tuple-element.256) | copy-start | bytes 983044
  186.2 5.3 collective-permute-start.6
  191.5 0.7 copy-start.7
  207.2 228.5 %collective-permute-start.7 = (bf16[64,2560]{1,0:T(8,128)(2,1)}, bf16[64,2560]{1,0:T(8,128)(2,1)S(1)}, u32[]{:S(2)}, u32[]{:S(2)}) collective-permute-start(bf16[64,2560]{1,0:T(8,128)(2,1)} %get-tuple-element.260), channel_id=1, source_target_pairs={{64,0},{96,32},{65,1},{97,33},{66,2},{98,34},{67,3},{99,35},{68,4}... | collective-permute-start | bytes 983048 | tf_op jit(solution)/shard_map/ppermute | solution.py:499
  435.7 0.7 copy-start.8
  484.6 30.4 %all-to-all-start.11 = ((bf16[32,16,2560]{2,1,0:T(8,128)(2,1)}), bf16[32,16,2560]{2,1,0:T(8,128)(2,1)S(1)}, u32[]{:S(2)}, u32[]{:S(2)}) async-start(bf16[32,16,2560]{2,1,0:T(8,128)(2,1)} %bitcast.143), calls=%async_computation.11 | async-start | bytes 5242880 | tf_op jit(solution)/shard_map/cond/branch_1_fun/all_to_all | solution.py:330
  565.4 5.2 copy-start.13
  565.4 25.5 %copy-start.1 = (bf16[64,2560]{1,0:T(8,128)(2,1)S(1)}, bf16[64,2560]{1,0:T(8,128)(2,1)}, u32[]{:S(2)}) copy-start(bf16[64,2560]{1,0:T(8,128)(2,1)} %get-tuple-element.232) | copy-start | bytes 983044 | tf_op jit(solution)/shard_map/cond
  565.4 25.5 %all-to-all-start.13 = ((bf16[32,16,2560]{2,1,0:T(8,128)(2,1)}), bf16[32,16,2560]{2,1,0:T(8,128)(2,1)S(1)}, u32[]{:S(2)}, u32[]{:S(2)}) async-start(bf16[32,16,2560]{2,1,0:T(8,128)(2,1)} %bitcast.142), calls=%async_computation.13 | async-start | bytes 5242880 | tf_op jit(solution)/shard_map/cond/branch_1_fun/all_to_all | solution.py:330
  595.1 2.2 collective-permute-start.8

commit v3 on v2

--- a/solution.py
+++ b/solution.py
@@ -12,26 +12,27 @@
 LAG_NANOS = 20000
 TURN_LAG_NANOS = 4000
 RETURN_LAG_NANOS = 4000
-AHEAD = 2
+FORWARD_AHEAD = 5
+BACKWARD_AHEAD = 3
 CONTRACT = (((1,), (1,)), ((), ()))
 IN_HBM = pl.BlockSpec(memory_space=pl.ANY)
 IN_SMEM = pl.BlockSpec(memory_space=pltpu.SMEM)
 IN_VMEM = pl.BlockSpec(memory_space=pltpu.VMEM)
 
 
-def late_kernel(nanos_ref, rows_ref, out_ref):
+def late_kernel(nanos_ref, anchor_ref, value_ref, out_ref):
     pl.delay(nanos_ref[0])
-    out_ref[...] = rows_ref[...]
-
-
-def held_back(rows, nanos):
+    out_ref[...] = value_ref[...]
+
+
+def held_back(anchor, value, nanos):
     return pl.pallas_call(
         late_kernel,
-        out_shape=jax.ShapeDtypeStruct(rows.shape, rows.dtype),
-        in_specs=[IN_SMEM, IN_VMEM],
+        out_shape=jax.ShapeDtypeStruct(value.shape, value.dtype),
+        in_specs=[IN_SMEM, IN_HBM, IN_VMEM],
         out_specs=IN_VMEM,
         name="held_back",
-    )(nanos.reshape(1), rows)
+    )(nanos.reshape(1), anchor, value)
 
 
 def fetch(pick, own, other, target, sem):
@@ -65,11 +66,12 @@
 
 
 class Incoming:
-    def __init__(self, starters):
+    def __init__(self, starters, ahead):
         self.starters = starters
+        self.ahead = ahead
         self.flying = []
         self.taken = 0
-        self.launch(1 + AHEAD)
+        self.launch(1 + ahead)
 
     def launch(self, upto):
         for start in self.starters[len(self.flying) : upto]:
@@ -79,7 +81,7 @@
         for _ in range(count):
             self.flying[self.taken].wait()
             self.taken += 1
-            self.launch(self.taken + 1 + AHEAD)
+            self.launch(self.taken + 1 + self.ahead)
 
 
 def pieces(total, widths):
@@ -95,12 +97,8 @@
     return parts
 
 
-def hidden_pieces(total):
-    return pieces(total, (256, 512))
-
-
 def feature_pieces(total):
-    return pieces(total, (1280, 768, 512))
+    return pieces(total, (512,) * (total // 512))
 
 
 def wide_dot(left, right):
@@ -124,27 +122,23 @@
     rows, gate, up, down, pre, val, act, out, in_sem, gate_sem, up_sem, down_sem, pre_sem, val_sem, out_sem,
 ):
     pick = pick_ref[0]
-    hidden_parts = hidden_pieces(gate.shape[1])
     feature_parts = feature_pieces(down.shape[1])
-    line = [brought(rows_hbm, rows, in_sem)]
-    for n, part in enumerate(hidden_parts):
-        line.append(fetch(pick, gate_a.at[:, part], gate_b.at[:, part], gate.at[:, part], gate_sem.at[n]))
-        line.append(fetch(pick, up_a.at[:, part], up_b.at[:, part], up.at[:, part], up_sem.at[n]))
+    line = []
+    for n, part in enumerate(feature_parts):
+        line.append(brought(rows_hbm.at[:, part], rows.at[:, part], in_sem.at[n]))
+        line.append(fetch(pick, gate_a.at[part, :], gate_b.at[part, :], gate.at[part, :], gate_sem.at[n]))
+        line.append(fetch(pick, up_a.at[part, :], up_b.at[part, :], up.at[part, :], up_sem.at[n]))
     for n, part in enumerate(feature_parts):
         line.append(fetch(pick, down_a.at[:, part], down_b.at[:, part], down.at[:, part], down_sem.at[n]))
-    incoming = Incoming(line)
-    incoming.take(1)
-    leaving = []
-    for n, part in enumerate(hidden_parts):
-        incoming.take(1)
-        gate_pre = wide_dot(rows[...], gate[:, part])
-        pre[:, part] = gate_pre
-        incoming.take(1)
-        up_val = wide_dot(rows[...], up[:, part])
-        val[:, part] = up_val
-        act[:, part] = (gate_pre * jax.nn.sigmoid(gate_pre) * up_val).astype(jnp.bfloat16)
-        leaving.append(started(pre.at[:, part], pre_hbm.at[:, part], pre_sem.at[n]))
-        leaving.append(started(val.at[:, part], val_hbm.at[:, part], val_sem.at[n]))
+    incoming = Incoming(line, FORWARD_AHEAD)
+    for n, part in enumerate(feature_parts):
+        incoming.take(3)
+        gate_part = wide_dot(rows[:, part], gate[part, :])
+        up_part = wide_dot(rows[:, part], up[part, :])
+        pre[...] = gate_part if n == 0 else pre[...] + gate_part
+        val[...] = up_part if n == 0 else val[...] + up_part
+    leaving = [started(pre, pre_hbm, pre_sem), started(val, val_hbm, val_sem)]
+    act[...] = (pre[...] * jax.nn.sigmoid(pre[...]) * val[...]).astype(jnp.bfloat16)
     for n, part in enumerate(feature_parts):
         incoming.take(1)
         out[:, part] = wide_dot(act[...], down[:, part]).astype(jnp.bfloat16)
@@ -155,7 +149,6 @@
 def expert_forward(pick, rows, own, other):
     slots, feat = rows.shape
     hidden = own[0].shape[1]
-    count = len(hidden_pieces(hidden))
     wide = len(feature_pieces(feat))
     bf16, f32 = jnp.bfloat16, jnp.float32
     return pl.pallas_call(
@@ -176,12 +169,12 @@
             pltpu.VMEM((slots, hidden), f32),
             pltpu.VMEM((slots, hidden), bf16),
             pltpu.VMEM((slots, feat), bf16),
+            pltpu.SemaphoreType.DMA((wide,)),
+            pltpu.SemaphoreType.DMA((wide,)),
+            pltpu.SemaphoreType.DMA((wide,)),
+            pltpu.SemaphoreType.DMA((wide,)),
             pltpu.SemaphoreType.DMA(()),
-            pltpu.SemaphoreType.DMA((count,)),
-            pltpu.SemaphoreType.DMA((count,)),
-            pltpu.SemaphoreType.DMA((wide,)),
-            pltpu.SemaphoreType.DMA((count,)),
-            pltpu.SemaphoreType.DMA((count,)),
+            pltpu.SemaphoreType.DMA(()),
             pltpu.SemaphoreType.DMA((wide,)),
         ],
         name="expert_forward",
@@ -191,28 +184,29 @@
 def backward_kernel(
     pick_ref, rows_hbm, pre_hbm, val_hbm, gate_a, up_a, down_a, gate_b, up_b, down_b,
     out_hbm,
-    rows, gate, up, down, pre, val, d_gate, d_up, out, in_sem, gate_sem, up_sem, down_sem, pre_sem, val_sem, out_sem,
+    rows, gate, up, down, pre, val, d_act, d_gate, d_up, out,
+    in_sem, gate_sem, up_sem, down_sem, pre_sem, val_sem, out_sem,
 ):
     pick = pick_ref[0]
-    hidden_parts = hidden_pieces(gate.shape[1])
     feature_parts = feature_pieces(down.shape[1])
-    line = [brought(rows_hbm, rows, in_sem)]
-    for n, part in enumerate(hidden_parts):
-        line.append(fetch(pick, down_a.at[part, :], down_b.at[part, :], down.at[part, :], down_sem.at[n]))
-        line.append(brought(pre_hbm.at[:, part], pre.at[:, part], pre_sem.at[n]))
-        line.append(brought(val_hbm.at[:, part], val.at[:, part], val_sem.at[n]))
+    line = []
+    for n, part in enumerate(feature_parts):
+        line.append(brought(rows_hbm.at[:, part], rows.at[:, part], in_sem.at[n]))
+        line.append(fetch(pick, down_a.at[:, part], down_b.at[:, part], down.at[:, part], down_sem.at[n]))
+    line.append(brought(pre_hbm, pre, pre_sem))
+    line.append(brought(val_hbm, val, val_sem))
     for n, part in enumerate(feature_parts):
         line.append(fetch(pick, gate_a.at[part, :], gate_b.at[part, :], gate.at[part, :], gate_sem.at[n]))
         line.append(fetch(pick, up_a.at[part, :], up_b.at[part, :], up.at[part, :], up_sem.at[n]))
-    incoming = Incoming(line)
-    incoming.take(1)
-    for part in hidden_parts:
-        incoming.take(1)
-        d_act = turned_dot(rows[...], down[part, :])
+    incoming = Incoming(line, BACKWARD_AHEAD)
+    for n, part in enumerate(feature_parts):
         incoming.take(2)
-        part_gate, part_up = gate_grads(d_act, pre[:, part], val[:, part])
-        d_gate[:, part] = part_gate
-        d_up[:, part] = part_up
+        partial = turned_dot(rows[:, part], down[:, part])
+        d_act[...] = partial if n == 0 else d_act[...] + partial
+    incoming.take(2)
+    part_gate, part_up = gate_grads(d_act[...], pre[...], val[...])
+    d_gate[...] = part_gate
+    d_up[...] = part_up
     leaving = []
     for n, part in enumerate(feature_parts):
         incoming.take(2)
@@ -225,7 +219,6 @@
 def expert_backward(pick, rows, pre, val, own, other):
     slots, feat = rows.shape
     hidden = own[0].shape[1]
-    count = len(hidden_pieces(hidden))
     wide = len(feature_pieces(feat))
     bf16, f32 = jnp.bfloat16, jnp.float32
     return pl.pallas_call(
@@ -240,15 +233,16 @@
             pltpu.VMEM((hidden, feat), bf16),
             pltpu.VMEM((slots, hidden), f32),
             pltpu.VMEM((slots, hidden), f32),
+            pltpu.VMEM((slots, hidden), f32),
             pltpu.VMEM((slots, hidden), bf16),
             pltpu.VMEM((slots, hidden), bf16),
             pltpu.VMEM((slots, feat), bf16),
+            pltpu.SemaphoreType.DMA((wide,)),
+            pltpu.SemaphoreType.DMA((wide,)),
+            pltpu.SemaphoreType.DMA((wide,)),
+            pltpu.SemaphoreType.DMA((wide,)),
             pltpu.SemaphoreType.DMA(()),
-            pltpu.SemaphoreType.DMA((wide,)),
-            pltpu.SemaphoreType.DMA((wide,)),
-            pltpu.SemaphoreType.DMA((count,)),
-            pltpu.SemaphoreType.DMA((count,)),
-            pltpu.SemaphoreType.DMA((count,)),
+            pltpu.SemaphoreType.DMA(()),
             pltpu.SemaphoreType.DMA((wide,)),
         ],
         name="expert_backward",
@@ -258,30 +252,29 @@
 def joint_kernel(
     pick_ref, rows_hbm, d_act_hbm, gate_a, up_a, gate_b, up_b,
     act_hbm, out_hbm,
-    rows, gate, up, d_act, act, d_gate, d_up, out, in_sem, gate_sem, up_sem, d_act_sem, act_sem, out_sem,
+    rows, gate, up, d_act, pre, val, act, d_gate, d_up, out, in_sem, gate_sem, up_sem, d_act_sem, act_sem, out_sem,
 ):
     pick = pick_ref[0]
-    hidden_parts = hidden_pieces(gate.shape[1])
     feature_parts = feature_pieces(out.shape[1])
-    line = [brought(rows_hbm, rows, in_sem)]
-    for n, part in enumerate(hidden_parts):
-        line.append(fetch(pick, gate_a.at[:, part], gate_b.at[:, part], gate.at[:, part], gate_sem.at[n]))
-        line.append(fetch(pick, up_a.at[:, part], up_b.at[:, part], up.at[:, part], up_sem.at[n]))
-        line.append(brought(d_act_hbm.at[:, part], d_act.at[:, part], d_act_sem.at[n]))
-    incoming = Incoming(line)
+    line = []
+    for n, part in enumerate(feature_parts):
+        line.append(brought(rows_hbm.at[:, part], rows.at[:, part], in_sem.at[n]))
+        line.append(fetch(pick, gate_a.at[part, :], gate_b.at[part, :], gate.at[part, :], gate_sem.at[n]))
+        line.append(fetch(pick, up_a.at[part, :], up_b.at[part, :], up.at[part, :], up_sem.at[n]))
+    line.append(brought(d_act_hbm, d_act, d_act_sem))
+    incoming = Incoming(line, FORWARD_AHEAD)
+    for n, part in enumerate(feature_parts):
+        incoming.take(3)
+        gate_part = wide_dot(rows[:, part], gate[part, :])
+        up_part = wide_dot(rows[:, part], up[part, :])
+        pre[...] = gate_part if n == 0 else pre[...] + gate_part
+        val[...] = up_part if n == 0 else val[...] + up_part
+    act[...] = (pre[...] * jax.nn.sigmoid(pre[...]) * val[...]).astype(jnp.bfloat16)
+    leaving = [started(act, act_hbm, act_sem)]
     incoming.take(1)
-    leaving = []
-    for n, part in enumerate(hidden_parts):
-        incoming.take(1)
-        gate_pre = wide_dot(rows[...], gate[:, part])
-        incoming.take(1)
-        up_val = wide_dot(rows[...], up[:, part])
-        act[:, part] = (gate_pre * jax.nn.sigmoid(gate_pre) * up_val).astype(jnp.bfloat16)
-        leaving.append(started(act.at[:, part], act_hbm.at[:, part], act_sem.at[n]))
-        incoming.take(1)
-        part_gate, part_up = gate_grads(d_act[:, part], gate_pre, up_val)
-        d_gate[:, part] = part_gate
-        d_up[:, part] = part_up
+    part_gate, part_up = gate_grads(d_act[...], pre[...], val[...])
+    d_gate[...] = part_gate
+    d_up[...] = part_up
     for n, part in enumerate(feature_parts):
         summed = turned_dot(d_gate[...], gate[part, :]) + turned_dot(d_up[...], up[part, :])
         out[:, part] = summed.astype(jnp.bfloat16)
@@ -292,7 +285,6 @@
 def expert_joint(pick, rows, d_act, own, other):
     slots, feat = rows.shape
     hidden = own[0].shape[1]
-    count = len(hidden_pieces(hidden))
     wide = len(feature_pieces(feat))
     bf16, f32 = jnp.bfloat16, jnp.float32
     return pl.pallas_call(
@@ -308,15 +300,17 @@
             pltpu.VMEM((feat, hidden), bf16),
             pltpu.VMEM((feat, hidden), bf16),
             pltpu.VMEM((slots, hidden), f32),
+            pltpu.VMEM((slots, hidden), f32),
+            pltpu.VMEM((slots, hidden), f32),
             pltpu.VMEM((slots, hidden), bf16),
             pltpu.VMEM((slots, hidden), bf16),
             pltpu.VMEM((slots, hidden), bf16),
             pltpu.VMEM((slots, feat), bf16),
+            pltpu.SemaphoreType.DMA((wide,)),
+            pltpu.SemaphoreType.DMA((wide,)),
+            pltpu.SemaphoreType.DMA((wide,)),
             pltpu.SemaphoreType.DMA(()),
-            pltpu.SemaphoreType.DMA((count,)),
-            pltpu.SemaphoreType.DMA((count,)),
-            pltpu.SemaphoreType.DMA((count,)),
-            pltpu.SemaphoreType.DMA((count,)),
+            pltpu.SemaphoreType.DMA(()),
             pltpu.SemaphoreType.DMA((wide,)),
         ],
         name="expert_joint",
@@ -443,8 +437,8 @@
     first_in = of_micro(inputs, mine)
     last_grad = of_micro(cotangent, mine)
     source = jnp.where(early, normed_rows(first_in, gain_low), last_grad)
-    source = held_back(source, jnp.where(mine == 1, LAG_NANOS, 0).astype(jnp.int32))
     picks_first = jnp.where(early, picks_low, picks_high)
+    picks_first = held_back(source, picks_first, jnp.where(mine == 1, LAG_NANOS, 0))
     scale_first = jnp.where(early, 1.0, scale_high)
     arrived = exchange((scale_first * spread(picks_first, source)).astype(jnp.bfloat16))
 
@@ -477,11 +471,14 @@
     )
     relayed = lax.ppermute(state_high, "segment", [(0, 2), (1, 3)])
 
-    relayed = held_back(relayed, jnp.where(mine == 1, TURN_LAG_NANOS, 0).astype(jnp.int32))
+    turn_gain = held_back(relayed, gain_low, jnp.where(mine == 1, TURN_LAG_NANOS, 0))
+    shared_state = lax.ppermute(
+        jnp.where(mine == 0, state_high, state_low), "segment", [(0, 1), (1, 0)]
+    )
 
     def turn(held):
-        layer_in, d_act = held
-        got_low = send_rows(layer_in, gain_low, picks_low)
+        layer_in, d_act, first_gain = held
+        got_low = send_rows(layer_in, first_gain, picks_low)
         out_low, pre_low, up_low = expert_forward(low_pick, got_low, own_mats, other_mats)
         state = mixed(layer_in, mix_low, exchange(out_low))
         got_high = send_rows(state, gain_high, picks_high)
@@ -495,13 +492,16 @@
     def stay(held):
         return no_rows, jnp.zeros((slots, hidden), jnp.bfloat16), no_rows, no_rows
 
-    turn_state, activated, turn_high, turn_low = lax.cond(early, stay, turn, (relayed, kept_a))
+    turn_state, activated, turn_high, turn_low = lax.cond(
+        early, stay, turn, (relayed, kept_a, turn_gain)
+    )
     came_back = lax.ppermute(turn_low, "segment", [(2, 0), (3, 1)])
 
-    came_back = held_back(came_back, jnp.where(mine == 1, RETURN_LAG_NANOS, 0).astype(jnp.int32))
-
-    def descend(dy):
-        d_got = send_grads(dy, picks_high, scale_high)
+    return_picks = held_back(came_back, picks_high, jnp.where(mine == 1, RETURN_LAG_NANOS, 0))
+
+    def descend(held):
+        dy, first_picks = held
+        d_got = send_grads(dy, first_picks, scale_high)
         d_rows_high = expert_backward(high_pick, d_got, kept_c, kept_d, own_mats, other_mats)
         grad_high = layer_grad(dy, state_low, gain_high, picks_high, exchange(d_rows_high))
         d_got_low = send_grads(grad_high, picks_low, scale_low)
@@ -509,25 +509,27 @@
         grad_low = layer_grad(grad_high, first_in, gain_low, picks_low, exchange(d_rows_low))
         return state_low, state_high, grad_low, grad_high
 
-    def finish(dy):
+    def finish(held):
         out_high = with_mats(1, lambda held, mats: project_down(held[0], mats[2]), activated)
         state = mixed(turn_state, mix_high, exchange(out_high))
         return turn_state, state, turn_low, turn_high
 
-    end_low, end_high, back_low, back_high = lax.cond(early, descend, finish, came_back)
-    kept = jnp.where(
-        mine == 0, jnp.stack([end_low, back_low]), jnp.stack([end_high, back_high])
-    )
-    given = jnp.where(
-        mine == 0, jnp.stack([end_high, back_high]), jnp.stack([end_low, back_low])
-    )
-    taken = swapped(given)
-    first = jnp.where(mine == 0, kept, taken)
-    second = jnp.where(mine == 0, taken, kept)
-    return (
-        jnp.stack([first[0], second[0]])[None],
-        jnp.stack([first[1], second[1]])[None],
-    )
+    end_low, end_high, back_low, back_high = lax.cond(
+        early, descend, finish, (came_back, return_picks)
+    )
+    other_grad = swapped(jnp.where(mine == 0, back_high, back_low))
+    late_state = lax.ppermute(
+        jnp.where(mine == 0, end_high, end_low), "segment", [(2, 3), (3, 2)]
+    )
+    other_state = jnp.where(early, shared_state, late_state)
+
+    def by_micro(low, high, other):
+        own = jnp.where(mine == 0, low, high)
+        first = jnp.where(mine == 0, own, other)
+        second = jnp.where(mine == 0, other, own)
+        return jnp.stack([first, second])[None]
+
+    return by_micro(end_low, end_high, other_state), by_micro(back_low, back_high, other_grad)
 
 
 def solution(mesh):

time: 611 us -> 578 us (0.946)
  waiting for transfers between devices: 345 us -> 321 us
  Pallas kernels: 87.9 us -> 72.3 us
    ppermute x1, waiting for transfers between devices: 227 us -> 209 us  [local(): came_back = lax.ppermute(turn_low, 'segment', [(2, 0), (3, 1)])]
    pallas_call x2, Pallas kernels: 32.2 us -> 25.9 us  [expert_backward(): pl.pallas_call(backward_kernel, out_shape=jax.ShapeDtypeStruct((slots, fe...]
  transfers between devices with their start and end apart: 14 -> 16, of which waited for: 8 -> 7; matrix products, arithmetic and copies ran while one was open for 2% -> 5% of each run, Pallas kernels for 4% -> 9%
where the time goes in v3:
time: 578 us; the launch traced here: 568 us
  waiting for transfers between devices  321 us (56%)
  blocking collectives  84.4 us (15%)
  Pallas kernels  72.3 us (13%)
  starting transfers between devices  36.6 us (6%)
  other arithmetic  19.1 us (3%)
  loops' own time  12.9 us (2%)
  matrix products  12.7 us (2%)
  local copies, waits for them, and re-layouts  7.61 us (1%)
    ppermute x1, waiting for transfers between devices, local(): came_back = lax.ppermute(turn_low, 'segment', [(2, 0), (3, 1)])  209 us
    all_to_all x5, waiting for transfers between devices, exchange(): lax.all_to_all(blocks, 'expert', split_axis=0, concat_axis=0, tiled=True)  107 us
    all_to_all x3, blocking collectives, exchange(): lax.all_to_all(blocks, 'expert', split_axis=0, concat_axis=0, tiled=True)  84.4 us
    all_to_all x5, starting transfers between devices, exchange(): lax.all_to_all(blocks, 'expert', split_axis=0, concat_axis=0, tiled=True)  28.5 us
    pallas_call x3, Pallas kernels, held_back(): pl.pallas_call(late_kernel, out_shape=jax.ShapeDtypeStruct(value.shape, v...  26.1 us
    pallas_call x2, Pallas kernels, expert_backward(): pl.pallas_call(backward_kernel, out_shape=jax.ShapeDtypeStruct((slots, fe...  25.9 us
    pallas_call x2, Pallas kernels, expert_forward(): pl.pallas_call(forward_kernel, out_shape=(jax.ShapeDtypeStruct((slots, fe...  20.4 us
    another operation x1, loops' own time, local(): lax.cond(early, stay, turn, (relayed, kept_a, turn_gain))  12 us
  transfers between devices with their start and end apart: 16, of which 7 were waited for; matrix products, arithmetic and copies ran while one was open for 5% of the time, Pallas kernels for 9%

profile of v3, /device:TPU:1, one launch (start us, length us, event | category | flops | bytes accessed | tf_op | source)
XLA Modules:
  0.0 567.8 jit_solution(8987891022407829114)
XLA Ops:
  0.6 1.5 collective-permute-start.2
  4.8 1.1 fusion.72
  7.6 1.1 select_reduce_fusion
  9.3 1.3 fusion.84
  10.6 2.0 fusion.75
  12.6 21.5 %held_back.3 = bf16[64,512]{1,0:T(8,128)(2,1)} custom-call(s32[1]{0:T(128)} %bitcast.49.nanos_ref, bf16[64,2560]{1,0:T(8,128)(2,1)} %get-tuple-element.289.anchor_ref, bf16[64,512]{1,0:T(8,128)(2,1)} %broadcast_select_fusion.6.value_ref), custom_call_target="tpu_custom_call" | custom-call | tf_op jit(solution)/shard_map/held_back/pallas_call | solution.py:29
  34.1 3.4 multiply_convert_fusion.3
  37.5 10.6 %all-to-all-start.14 = ((bf16[32,16,2560]{2,1,0:T(8,128)(2,1)}), bf16[32,16,2560]{2,1,0:T(8,128)(2,1)S(1)}, u32[]{:S(2)}, u32[]{:S(2)}) async-start(bf16[32,16,2560]{2,1,0:T(8,128)(2,1)} %bitcast.52), calls=%async_computation.14 | async-start | bytes 5242880 | tf_op jit(solution)/shard_map/all_to_all | solution.py:324
  48.2 21.3 %all-to-all-done.14 = bf16[32,16,2560]{2,1,0:T(8,128)(2,1)S(1)} async-done(((bf16[32,16,2560]{2,1,0:T(8,128)(2,1)}), bf16[32,16,2560]{2,1,0:T(8,128)(2,1)S(1)}, u32[]{:S(2)}, u32[]{:S(2)}) %all-to-all-start.14) | async-done | bytes 2621472 | tf_op jit(solution)/shard_map/all_to_all | solution.py:324
  69.5 113.4 %conditional.9 = (bf16[64,2560]{1,0:T(8,128)(2,1)}, bf16[64,2560]{1,0:T(8,128)(2,1)S(1)}, f32[512,768]{1,0:T(8,128)}, f32[512,768]{1,0:T(8,128)}, f32[512,768]{1,0:T(8,128)}, /*index=5*/f32[512,768]{1,0:T(8,128)}) conditional(s32[]{:T(128)} %convert_element_type.164, (s32[]{:T(128)}, bf16[512,2560]{1,0:T(8,128)(2,1)S(1)}, ...), branch_computations={%region_8.11_spmd, %region_11.13_spmd} | conditional | flops 2013265920 | bytes 37166252 | solution.py:469
  69.5 10.1 %expert_forward.3 = (bf16[512,2560]{1,0:T(8,128)(2,1)}, f32[512,768]{1,0:T(8,128)}, f32[512,768]{1,0:T(8,128)}) custom-call(s32[1]{0:T(128)} %bitcast.pick_ref, bf16[512,2560]{1,0:T(8,128)(2,1)S(1)} %get-tuple-element.170.rows_hbm, bf16[2560,768]{1,0:T(8,128)(2,1)} %get-tuple-element.171.gate_a, bf16[2560,768]{1,0:T(8,128)(2,1)} %get-tuple-element.172.up_a, ...), custom_call_target="tpu_custom_call" | custom-call | tf_op jit(solution)/shard_map/cond/branch_1_fun/expert_forward/pallas_call | solution.py:154
  79.7 5.3 all-to-all-start
  85.1 21.9 %all-to-all-done = bf16[32,16,2560]{2,1,0:T(8,128)(2,1)S(1)} async-done(((bf16[32,16,2560]{2,1,0:T(8,128)(2,1)}), bf16[32,16,2560]{2,1,0:T(8,128)(2,1)S(1)}, u32[]{:S(2)}, u32[]{:S(2)}) %all-to-all-start) | async-done | bytes 2621472 | tf_op jit(solution)/shard_map/cond/branch_1_fun/all_to_all | solution.py:324
  107.5 0.9 fusion.8
  108.5 1.9 convolution_convert_fusion
  110.4 32.3 %all_to_all.61 = bf16[32,16,2560]{2,1,0:T(8,128)(2,1)} all-to-all(bf16[32,16,2560]{2,1,0:T(8,128)(2,1)S(1)} %bitcast.157), channel_id=1, replica_groups=mesh['segment'=4,'expert'=32] {'expert'}, dimensions={0} | all-to-all | bytes 5242880 | tf_op jit(solution)/shard_map/cond/branch_1_fun/all_to_all | solution.py:324
  142.6 10.2 %expert_forward.4 = (bf16[512,2560]{1,0:T(8,128)(2,1)}, f32[512,768]{1,0:T(8,128)}, f32[512,768]{1,0:T(8,128)}) custom-call(s32[1]{0:T(128)} %bitcast.3.pick_ref, bf16[512,2560]{1,0:T(8,128)(2,1)} %bitcast.165, bf16[2560,768]{1,0:T(8,128)(2,1)} %get-tuple-element.171.gate_a, bf16[2560,768]{1,0:T(8,128)(2,1)} %get-tuple-element.172.up_a, ...), custom_call_target="tpu_custom_call" | custom-call | tf_op jit(solution)/shard_map/cond/branch_1_fun/expert_forward/pallas_call | solution.py:154
  152.9 4.1 all-to-all-start.2
  157.0 23.9 %all-to-all-done.2 = bf16[32,16,2560]{2,1,0:T(8,128)(2,1)S(1)} async-done(((bf16[32,16,2560]{2,1,0:T(8,128)(2,1)}), bf16[32,16,2560]{2,1,0:T(8,128)(2,1)S(1)}, u32[]{:S(2)}, u32[]{:S(2)}) %all-to-all-start.2) | async-done | bytes 2621472 | tf_op jit(solution)/shard_map/cond/branch_1_fun/all_to_all | solution.py:324
  181.4 1.1 fusion.11
  182.9 1.3 collective-permute-start.6
  184.2 4.0 collective-permute-done.6.anchor_ref
  188.2 14.5 %conditional.10 = (bf16[64,2560]{1,0:T(8,128)(2,1)S(1)}, bf16[512,768]{1,0:T(8,128)(2,1)}, bf16[64,2560]{1,0:T(8,128)(2,1)}, bf16[64,2560]{1,0:T(8,128)(2,1)}) conditional(s32[]{:T(128)} %convert_element_type.164, (bf16[64,2560]{1,0:T(8,128)(2,1)S(1)}, f32[64,512]{1,0:T(8,128)}, s32[]{:T(128)}, f32[1,2560]{1,0:T(1,128)S(1)}, ...), branch_computations={%region_14.19_spmd, %region_19.20_spmd} | conditional | flops 1186922752 | bytes 65049364 | solution.py:495
  200.3 0.9 broadcast.164
  202.7 1.3 collective-permute-start.7
  204.0 1.8 broadcast_select_fusion.4
  205.7 1.9 collective-permute-start.8
  207.7 209.5 %collective-permute-done.7.anchor_ref = bf16[64,2560]{1,0:T(8,128)(2,1)S(1)} collective-permute-done((bf16[64,2560]{1,0:T(8,128)(2,1)}, bf16[64,2560]{1,0:T(8,128)(2,1)S(1)}, u32[]{:S(2)}, u32[]{:S(2)}) %collective-permute-start.7) | collective-permute-done | bytes 327712 | tf_op jit(solution)/shard_map/ppermute | solution.py:498
  417.1 4.6 held_back.5
  421.7 139.7 %conditional.11 = (bf16[64,2560]{1,0:T(8,128)(2,1)S(1)}, bf16[64,2560]{1,0:T(8,128)(2,1)}, bf16[64,2560]{1,0:T(8,128)(2,1)}, bf16[64,2560]{1,0:T(8,128)(2,1)}) conditional(s32[]{:T(128)} %convert_element_type.164, (bf16[64,2560]{1,0:T(8,128)(2,1)S(1)}, f32[64,512]{1,0:T(8,128)S(1)}, s32[]{:T(128)}, bf16[512,768]{1,0:T(8,128)(2,1)}, ...), branch_computations={%region_20.23_spmd, %region_23.28_spmd} | conditional | flops 2349858816 | bytes 45593760 | solution.py:517
  421.7 1.7 multiply_convert_fusion.2
  423.5 25.5 %all_to_all.66 = bf16[32,16,2560]{2,1,0:T(8,128)(2,1)} all-to-all(bf16[32,16,2560]{2,1,0:T(8,128)(2,1)S(1)} %bitcast.161), channel_id=1, replica_groups=mesh['segment'=4,'expert'=32] {'expert'}, dimensions={0} | all-to-all | bytes 5242880 | tf_op jit(solution)/shard_map/cond/branch_1_fun/all_to_all | solution.py:324
  448.9 12.9 %expert_backward.4 = bf16[512,2560]{1,0:T(8,128)(2,1)} custom-call(s32[1]{0:T(128)} %bitcast.31.pick_ref, bf16[512,2560]{1,0:T(8,128)(2,1)} %bitcast.147, f32[512,768]{1,0:T(8,128)} %get-tuple-element.229.pre_hbm, f32[512,768]{1,0:T(8,128)} %get-tuple-element.230.val_hbm, bf16[2560,768]{1,0:T(8,128)(2,1)} %get-tuple-element.231.gate_a, ...), custom_call_target="tpu_custom_call" | custom-call | tf_op jit(solution)/shard_map/cond/branch_1_fun/expert_backward/pallas_call | solution.py:224
  461.9 4.3 all-to-all-start.11
  466.2 21.4 %all-to-all-done.11 = bf16[32,16,2560]{2,1,0:T(8,128)(2,1)S(1)} async-done(((bf16[32,16,2560]{2,1,0:T(8,128)(2,1)}), bf16[32,16,2560]{2,1,0:T(8,128)(2,1)S(1)}, u32[]{:S(2)}, u32[]{:S(2)}) %all-to-all-start.11) | async-done | bytes 2621472 | tf_op jit(solution)/shard_map/cond/branch_1_fun/all_to_all | solution.py:324
  487.6 1.6 fusion.60
  489.3 2.0 fusion.63
  491.2 1.9 multiply_convert_fusion.1
  493.1 26.7 %all_to_all.67 = bf16[32,16,2560]{2,1,0:T(8,128)(2,1)} all-to-all(bf16[32,16,2560]{2,1,0:T(8,128)(2,1)S(1)} %bitcast.162), channel_id=1, replica_groups=mesh['segment'=4,'expert'=32] {'expert'}, dimensions={0} | all-to-all | bytes 5242880 | tf_op jit(solution)/shard_map/cond/branch_1_fun/all_to_all | solution.py:324
  519.8 12.9 %expert_backward.5 = bf16[512,2560]{1,0:T(8,128)(2,1)} custom-call(s32[1]{0:T(128)} %bitcast.37.pick_ref, bf16[512,2560]{1,0:T(8,128)(2,1)} %bitcast.148, f32[512,768]{1,0:T(8,128)} %get-tuple-element.243.pre_hbm, f32[512,768]{1,0:T(8,128)} %get-tuple-element.244.val_hbm, bf16[2560,768]{1,0:T(8,128)(2,1)} %get-tuple-element.231.gate_a, ...), custom_call_target="tpu_custom_call" | custom-call | tf_op jit(solution)/shard_map/cond/branch_1_fun/expert_backward/pallas_call | solution.py:224
  532.7 4.2 all-to-all-start.13
  537.0 1.0 copy.82
  537.9 1.7 copy.83
  539.7 18.8 %all-to-all-done.13 = bf16[32,16,2560]{2,1,0:T(8,128)(2,1)S(1)} async-done(((bf16[32,16,2560]{2,1,0:T(8,128)(2,1)}), bf16[32,16,2560]{2,1,0:T(8,128)(2,1)S(1)}, u32[]{:S(2)}, u32[]{:S(2)}) %all-to-all-start.13) | async-done | bytes 2621472 | tf_op jit(solution)/shard_map/cond/branch_1_fun/all_to_all | solution.py:324
  559.2 2.0 fusion.68
  562.2 1.0 broadcast_select_fusion.1
  563.3 1.2 select_bitcast_fusion.3
  565.4 1.0 select_bitcast_fusion.1
  (72 shorter events, 10.9 us)
Async XLA Ops:
  0.6 8.7 %collective-permute-start.2 = (f32[1,2560]{1,0:T(1,128)}, f32[1,2560]{1,0:T(1,128)S(1)}, u32[]{:S(2)}, u32[]{:S(2)}) collective-permute-start(f32[1,2560]{1,0:T(1,128)} %param.20), channel_id=1, source_target_pairs={{0,32},{32,0},{64,96},{96,64},{1,33},{33,1},{65,97},{97,65},{2,34}... | collective-permute-start | bytes 30728 | tf_op jit(solution)/shard_map/ppermute | solution.py:401
  2.9 4.7 collective-permute-start.1
  3.8 2.2 collective-permute-start
  4.3 65.2 %collective-permute-start.3 = (bf16[768,2560]{1,0:T(8,128)(2,1)}, bf16[768,2560]{1,0:T(8,128)(2,1)}, u32[]{:S(2)}, u32[]{:S(2)}) collective-permute-start(bf16[768,2560]{1,0:T(8,128)(2,1)} %bitcast.137), channel_id=1, source_target_pairs={{0,32},{32,0},{64,96},{96,64},{1,33},{33,1},{65,97},{97,65},{2,34}... | collective-permute-start | bytes 11796488 | tf_op jit(solution)/shard_map/ppermute | solution.py:401
  4.4 65.1 %collective-permute-start.4 = (bf16[2560,768]{1,0:T(8,128)(2,1)}, bf16[2560,768]{1,0:T(8,128)(2,1)}, u32[]{:S(2)}, u32[]{:S(2)}) collective-permute-start(bf16[2560,768]{1,0:T(8,128)(2,1)} %bitcast.129), channel_id=1, source_target_pairs={{0,32},{32,0},{64,96},{96,64},{1,33},{33,1},{65,97},{97,65},{2,34}... | collective-permute-start | bytes 11796488 | tf_op jit(solution)/shard_map/ppermute | solution.py:401
  6.0 63.5 %copy-start = (bf16[64,2560]{1,0:T(8,128)(2,1)}, bf16[64,2560]{1,0:T(8,128)(2,1)S(1)}, u32[]{:S(2)}) copy-start(bf16[64,2560]{1,0:T(8,128)(2,1)S(1)} %get-tuple-element.292) | copy-start | bytes 983044
  6.0 63.5 %collective-permute-start.5 = (bf16[2560,768]{1,0:T(8,128)(2,1)}, bf16[2560,768]{1,0:T(8,128)(2,1)}, u32[]{:S(2)}, u32[]{:S(2)}) collective-permute-start(bf16[2560,768]{1,0:T(8,128)(2,1)} %bitcast.133), channel_id=1, source_target_pairs={{0,32},{32,0},{64,96},{96,64},{1,33},{33,1},{65,97},{97,65},{2,34}... | collective-permute-start | bytes 11796488 | tf_op jit(solution)/shard_map/ppermute | solution.py:401
  8.7 0.6 copy-start.12
  37.5 32.0 %all-to-all-start.14 = ((bf16[32,16,2560]{2,1,0:T(8,128)(2,1)}), bf16[32,16,2560]{2,1,0:T(8,128)(2,1)S(1)}, u32[]{:S(2)}, u32[]{:S(2)}) async-start(bf16[32,16,2560]{2,1,0:T(8,128)(2,1)} %bitcast.52), calls=%async_computation.14 | async-start | bytes 5242880 | tf_op jit(solution)/shard_map/all_to_all | solution.py:324
  79.7 5.3 copy-start.7
  79.7 5.4 copy-start.5
  79.7 27.3 %all-to-all-start = ((bf16[32,16,2560]{2,1,0:T(8,128)(2,1)}), bf16[32,16,2560]{2,1,0:T(8,128)(2,1)S(1)}, u32[]{:S(2)}, u32[]{:S(2)}) async-start(bf16[32,16,2560]{2,1,0:T(8,128)(2,1)} %bitcast.168), calls=%async_computation | async-start | bytes 5242880 | tf_op jit(solution)/shard_map/cond/branch_1_fun/all_to_all | solution.py:324
  152.9 28.0 %all-to-all-start.2 = ((bf16[32,16,2560]{2,1,0:T(8,128)(2,1)}), bf16[32,16,2560]{2,1,0:T(8,128)(2,1)S(1)}, u32[]{:S(2)}, u32[]{:S(2)}) async-start(bf16[32,16,2560]{2,1,0:T(8,128)(2,1)} %bitcast.170), calls=%async_computation.2 | async-start | bytes 5242880 | tf_op jit(solution)/shard_map/cond/branch_1_fun/all_to_all | solution.py:324
  182.9 5.3 copy-start.2
  182.9 5.3 collective-permute-start.6
  202.7 214.4 %collective-permute-start.7 = (bf16[64,2560]{1,0:T(8,128)(2,1)}, bf16[64,2560]{1,0:T(8,128)(2,1)S(1)}, u32[]{:S(2)}, u32[]{:S(2)}) collective-permute-start(bf16[64,2560]{1,0:T(8,128)(2,1)} %get-tuple-element.265), channel_id=1, source_target_pairs={{64,0},{96,32},{65,1},{97,33},{66,2},{98,34},{67,3},{99,35},{68,4}... | collective-permute-start | bytes 983048 | tf_op jit(solution)/shard_map/ppermute | solution.py:498
  205.7 357.6 %collective-permute-start.8 = (bf16[64,2560]{1,0:T(8,128)(2,1)}, bf16[64,2560]{1,0:T(8,128)(2,1)}, u32[]{:S(2)}, u32[]{:S(2)}) collective-permute-start(bf16[64,2560]{1,0:T(8,128)(2,1)} %broadcast_select_fusion.4), channel_id=1, source_target_pairs={{0,32},{32,0},{1,33},{33,1},{2,34},{34,2},{3,35},{35,3},{4,36},{36... | collective-permute-start | bytes 983048 | tf_op jit(solution)/shard_map/ppermute | solution.py:475
  461.8 4.3 copy-start.9
  461.9 25.8 %all-to-all-start.11 = ((bf16[32,16,2560]{2,1,0:T(8,128)(2,1)}), bf16[32,16,2560]{2,1,0:T(8,128)(2,1)S(1)}, u32[]{:S(2)}, u32[]{:S(2)}) async-start(bf16[32,16,2560]{2,1,0:T(8,128)(2,1)} %bitcast.145), calls=%async_computation.11 | async-start | bytes 5242880 | tf_op jit(solution)/shard_map/cond/branch_1_fun/all_to_all | solution.py:324
  532.7 25.8 %copy-start.1 = (bf16[64,2560]{1,0:T(8,128)(2,1)S(1)}, bf16[64,2560]{1,0:T(8,128)(2,1)}, u32[]{:S(2)}) copy-start(bf16[64,2560]{1,0:T(8,128)(2,1)} %get-tuple-element.238) | copy-start | bytes 983044 | tf_op jit(solution)/shard_map/cond
  532.7 25.8 %all-to-all-start.13 = ((bf16[32,16,2560]{2,1,0:T(8,128)(2,1)}), bf16[32,16,2560]{2,1,0:T(8,128)(2,1)S(1)}, u32[]{:S(2)}, u32[]{:S(2)}) async-start(bf16[32,16,2560]{2,1,0:T(8,128)(2,1)} %bitcast.143), calls=%async_computation.13 | async-start | bytes 5242880 | tf_op jit(solution)/shard_map/cond/branch_1_fun/all_to_all | solution.py:324
  561.5 1.8 collective-permute-start.9
  563.2 2.2 collective-permute-start.10

commit v4 on v3

--- a/solution.py
+++ b/solution.py
@@ -11,9 +11,9 @@
 
 LAG_NANOS = 20000
 TURN_LAG_NANOS = 4000
-RETURN_LAG_NANOS = 4000
+RETURN_LAG_NANOS = 1500
 FORWARD_AHEAD = 5
-BACKWARD_AHEAD = 3
+FEATURE_STEP = 512
 CONTRACT = (((1,), (1,)), ((), ()))
 IN_HBM = pl.BlockSpec(memory_space=pl.ANY)
 IN_SMEM = pl.BlockSpec(memory_space=pltpu.SMEM)
@@ -35,16 +35,19 @@
     )(nanos.reshape(1), anchor, value)
 
 
+def launch(pick, own, other, target, sem):
+    @pl.when(pick == 0)
+    def _():
+        pltpu.make_async_copy(own, target, sem).start()
+
+    @pl.when(pick != 0)
+    def _():
+        pltpu.make_async_copy(other, target, sem).start()
+
+
 def fetch(pick, own, other, target, sem):
     def start():
-        @pl.when(pick == 0)
-        def _():
-            pltpu.make_async_copy(own, target, sem).start()
-
-        @pl.when(pick != 0)
-        def _():
-            pltpu.make_async_copy(other, target, sem).start()
-
+        launch(pick, own, other, target, sem)
         return pltpu.make_async_copy(own, target, sem)
 
     return start
@@ -99,6 +102,45 @@
 
 def feature_pieces(total):
     return pieces(total, (512,) * (total // 512))
+
+
+def arrive(source, target, sem):
+    pltpu.make_async_copy(source, target, sem).wait()
+
+
+def block(n):
+    return pl.ds(pl.multiple_of(n * FEATURE_STEP, FEATURE_STEP), FEATURE_STEP)
+
+
+def staged(count, first, later, work):
+    for n in range(2):
+        first(n)
+
+    def step(n, carry):
+        @pl.when(n + 2 < count)
+        def _():
+            first(n + 2)
+
+        @pl.when(n + 2 >= count)
+        def _():
+            later(n + 2 - count)
+
+        work(n)
+        return carry
+
+    lax.fori_loop(0, count, step, 0)
+
+
+def continued(count, first, work):
+    def step(n, carry):
+        @pl.when(n + 2 < count)
+        def _():
+            first(n + 2)
+
+        work(n)
+        return carry
+
+    lax.fori_loop(0, count, step, 0)
 
 
 def wide_dot(left, right):
@@ -188,32 +230,48 @@
     in_sem, gate_sem, up_sem, down_sem, pre_sem, val_sem, out_sem,
 ):
     pick = pick_ref[0]
-    feature_parts = feature_pieces(down.shape[1])
-    line = []
-    for n, part in enumerate(feature_parts):
-        line.append(brought(rows_hbm.at[:, part], rows.at[:, part], in_sem.at[n]))
-        line.append(fetch(pick, down_a.at[:, part], down_b.at[:, part], down.at[:, part], down_sem.at[n]))
-    line.append(brought(pre_hbm, pre, pre_sem))
-    line.append(brought(val_hbm, val, val_sem))
-    for n, part in enumerate(feature_parts):
-        line.append(fetch(pick, gate_a.at[part, :], gate_b.at[part, :], gate.at[part, :], gate_sem.at[n]))
-        line.append(fetch(pick, up_a.at[part, :], up_b.at[part, :], up.at[part, :], up_sem.at[n]))
-    incoming = Incoming(line, BACKWARD_AHEAD)
-    for n, part in enumerate(feature_parts):
-        incoming.take(2)
-        partial = turned_dot(rows[:, part], down[:, part])
-        d_act[...] = partial if n == 0 else d_act[...] + partial
-    incoming.take(2)
+    count = down.shape[1] // FEATURE_STEP
+
+    def first(n):
+        part = block(n)
+        started(rows_hbm.at[:, part], rows.at[:, part], in_sem.at[n])
+        launch(pick, down_a.at[:, part], down_b.at[:, part], down.at[:, part], down_sem.at[n])
+
+    def second(n):
+        part = block(n)
+        launch(pick, gate_a.at[part, :], gate_b.at[part, :], gate.at[part, :], gate_sem.at[n])
+        launch(pick, up_a.at[part, :], up_b.at[part, :], up.at[part, :], up_sem.at[n])
+
+    def widen(n):
+        part = block(n)
+
+        @pl.when(n == 1)
+        def _():
+            started(pre_hbm, pre, pre_sem)
+            started(val_hbm, val, val_sem)
+
+        arrive(rows_hbm.at[:, part], rows.at[:, part], in_sem.at[n])
+        arrive(down_a.at[:, part], down.at[:, part], down_sem.at[n])
+        d_act[...] += turned_dot(rows[:, part], down[:, part])
+
+    def narrow(n):
+        part = block(n)
+        arrive(gate_a.at[part, :], gate.at[part, :], gate_sem.at[n])
+        arrive(up_a.at[part, :], up.at[part, :], up_sem.at[n])
+        summed = turned_dot(d_gate[...], gate[part, :]) + turned_dot(d_up[...], up[part, :])
+        out[:, part] = summed.astype(jnp.bfloat16)
+        started(out.at[:, part], out_hbm.at[:, part], out_sem.at[n])
+
+    d_act[...] = jnp.zeros_like(d_act)
+    staged(count, first, second, widen)
+    arrive(pre_hbm, pre, pre_sem)
+    arrive(val_hbm, val, val_sem)
     part_gate, part_up = gate_grads(d_act[...], pre[...], val[...])
     d_gate[...] = part_gate
     d_up[...] = part_up
-    leaving = []
-    for n, part in enumerate(feature_parts):
-        incoming.take(2)
-        summed = turned_dot(d_gate[...], gate[part, :]) + turned_dot(d_up[...], up[part, :])
-        out[:, part] = summed.astype(jnp.bfloat16)
-        leaving.append(started(out.at[:, part], out_hbm.at[:, part], out_sem.at[n]))
-    wait_all(leaving)
+    continued(count, second, narrow)
+    for n in range(count):
+        arrive(out.at[:, block(n)], out_hbm.at[:, block(n)], out_sem.at[n])
 
 
 def expert_backward(pick, rows, pre, val, own, other):
@@ -429,18 +487,33 @@
     low_pick = mine.astype(jnp.int32)
     high_pick = 1 - low_pick
 
-    picks_low, mix_low = slot_matrices(route_low, gate_low, experts, capacity)
-    picks_high, mix_high = slot_matrices(route_high, gate_high, experts, capacity)
-    scale_low = jnp.sum(mix_low, axis=0)[:, None]
-    scale_high = jnp.sum(mix_high, axis=0)[:, None]
-
+    picks_first, mix_first = slot_matrices(
+        jnp.where(early, route_low, route_high),
+        jnp.where(early, gate_low, gate_high),
+        experts,
+        capacity,
+    )
+    scale_first = jnp.where(early, 1.0, jnp.sum(mix_first, axis=0))[:, None]
     first_in = of_micro(inputs, mine)
     last_grad = of_micro(cotangent, mine)
     source = jnp.where(early, normed_rows(first_in, gain_low), last_grad)
-    picks_first = jnp.where(early, picks_low, picks_high)
-    picks_first = held_back(source, picks_first, jnp.where(mine == 1, LAG_NANOS, 0))
-    scale_first = jnp.where(early, 1.0, scale_high)
-    arrived = exchange((scale_first * spread(picks_first, source)).astype(jnp.bfloat16))
+    picks_held = held_back(source, picks_first, jnp.where(mine == 1, LAG_NANOS, 0))
+    outgoing = (scale_first * spread(picks_held, source)).astype(jnp.bfloat16)
+    outgoing, route_next, gate_next = lax.optimization_barrier(
+        (
+            outgoing,
+            jnp.where(early, route_high, route_low),
+            jnp.where(early, gate_high, gate_low),
+        )
+    )
+    arrived = exchange(outgoing)
+    picks_next, mix_next = slot_matrices(route_next, gate_next, experts, capacity)
+    picks_low = jnp.where(early, picks_first, picks_next)
+    picks_high = jnp.where(early, picks_next, picks_first)
+    mix_low = jnp.where(early, mix_first, mix_next)
+    mix_high = jnp.where(early, mix_next, mix_first)
+    scale_low = jnp.sum(mix_low, axis=0)[:, None]
+    scale_high = jnp.sum(mix_high, axis=0)[:, None]
 
     def send_rows(layer_in, gain, picks):
         return exchange(spread(picks, normed_rows(layer_in, gain)).astype(jnp.bfloat16))
@@ -472,9 +545,6 @@
     relayed = lax.ppermute(state_high, "segment", [(0, 2), (1, 3)])
 
     turn_gain = held_back(relayed, gain_low, jnp.where(mine == 1, TURN_LAG_NANOS, 0))
-    shared_state = lax.ppermute(
-        jnp.where(mine == 0, state_high, state_low), "segment", [(0, 1), (1, 0)]
-    )
 
     def turn(held):
         layer_in, d_act, first_gain = held
@@ -517,19 +587,14 @@
     end_low, end_high, back_low, back_high = lax.cond(
         early, descend, finish, (came_back, return_picks)
     )
-    other_grad = swapped(jnp.where(mine == 0, back_high, back_low))
-    late_state = lax.ppermute(
-        jnp.where(mine == 0, end_high, end_low), "segment", [(2, 3), (3, 2)]
-    )
-    other_state = jnp.where(early, shared_state, late_state)
-
-    def by_micro(low, high, other):
-        own = jnp.where(mine == 0, low, high)
-        first = jnp.where(mine == 0, own, other)
-        second = jnp.where(mine == 0, other, own)
-        return jnp.stack([first, second])[None]
-
-    return by_micro(end_low, end_high, other_state), by_micro(back_low, back_high, other_grad)
+    low = jnp.stack([end_low, back_low])
+    high = jnp.stack([end_high, back_high])
+    other = swapped(jnp.where(mine == 0, high, low))
+    own = jnp.where(mine == 0, low, high)
+    is_mine = jnp.arange(micro_count)[:, None, None] == mine
+    all_states = jnp.where(is_mine, own[0][None], other[0][None])[None]
+    all_grads = jnp.where(is_mine, own[1][None], other[1][None])[None]
+    return all_states, all_grads
 
 
 def solution(mesh):

time: 578 us -> 571 us (0.988)
  transfers between devices with their start and end apart: 16 -> 14, of which waited for: 7 -> 8; matrix products, arithmetic and copies ran while one was open for 5% -> 3% of each run, Pallas kernels for 9% -> 4%
where the time goes in v4:
time: 571 us; the launch traced here: 561 us
  waiting for transfers between devices  324 us (57%)
  blocking collectives  84.5 us (15%)
  Pallas kernels  68.1 us (12%)
  starting transfers between devices  33.9 us (6%)
  other arithmetic  15.4 us (3%)
  loops' own time  13.8 us (2%)
  matrix products  12.6 us (2%)
  local copies, waits for them, and re-layouts  7.7 us (1%)
    ppermute x1, waiting for transfers between devices, local(): came_back = lax.ppermute(turn_low, 'segment', [(2, 0), (3, 1)])  212 us
    all_to_all x5, waiting for transfers between devices, exchange(): lax.all_to_all(blocks, 'expert', split_axis=0, concat_axis=0, tiled=True)  106 us
    all_to_all x3, blocking collectives, exchange(): lax.all_to_all(blocks, 'expert', split_axis=0, concat_axis=0, tiled=True)  84.5 us
    all_to_all x5, starting transfers between devices, exchange(): lax.all_to_all(blocks, 'expert', split_axis=0, concat_axis=0, tiled=True)  28.4 us
    pallas_call x2, Pallas kernels, expert_backward(): pl.pallas_call(backward_kernel, out_shape=jax.ShapeDtypeStruct((slots, fe...  24.2 us
    pallas_call x3, Pallas kernels, held_back(): pl.pallas_call(late_kernel, out_shape=jax.ShapeDtypeStruct(value.shape, v...  23.6 us
    pallas_call x2, Pallas kernels, expert_forward(): pl.pallas_call(forward_kernel, out_shape=(jax.ShapeDtypeStruct((slots, fe...  20.3 us
    another operation x1, loops' own time, local(): lax.cond(early, stay, turn, (relayed, kept_a, turn_gain))  13.2 us
  transfers between devices with their start and end apart: 14, of which 8 were waited for; matrix products, arithmetic and copies ran while one was open for 3% of the time, Pallas kernels for 4%

profile of v4, /device:TPU:1, one launch (start us, length us, event | category | flops | bytes accessed | tf_op | source)
XLA Modules:
  0.0 561.5 jit_solution(11357504733182365216)
XLA Ops:
  0.6 1.5 collective-permute-start.2
  2.1 0.8 constant_dynamic-slice_fusion.3
  3.0 0.8 constant_dynamic-slice_fusion.1
  4.8 1.1 fusion.73
  6.9 0.8 select_reduce_fusion
  7.7 1.3 fusion.90
  9.1 2.0 fusion.76
  11.0 21.5 %held_back.3 = bf16[64,512]{1,0:T(8,128)(2,1)} custom-call(s32[1]{0:T(128)} %bitcast.51.nanos_ref, bf16[64,2560]{1,0:T(8,128)(2,1)} %get-tuple-element.299.anchor_ref, bf16[64,512]{1,0:T(8,128)(2,1)} %get-tuple-element.292.value_ref), custom_call_target="tpu_custom_call" | custom-call | tf_op jit(solution)/shard_map/held_back/pallas_call | solution.py:29
  32.5 3.4 multiply_convert_fusion.3
  35.9 10.8 %all-to-all-start.14 = ((bf16[32,16,2560]{2,1,0:T(8,128)(2,1)}), bf16[32,16,2560]{2,1,0:T(8,128)(2,1)S(1)}, u32[]{:S(2)}, u32[]{:S(2)}) async-start(bf16[32,16,2560]{2,1,0:T(8,128)(2,1)} %bitcast.54), calls=%async_computation.14 | async-start | bytes 5242880 | tf_op jit(solution)/shard_map/all_to_all | solution.py:382
  48.3 19.7 %all-to-all-done.14 = bf16[32,16,2560]{2,1,0:T(8,128)(2,1)S(1)} async-done(((bf16[32,16,2560]{2,1,0:T(8,128)(2,1)}), bf16[32,16,2560]{2,1,0:T(8,128)(2,1)S(1)}, u32[]{:S(2)}, u32[]{:S(2)}) %all-to-all-start.14) | async-done | bytes 2621472 | tf_op jit(solution)/shard_map/all_to_all | solution.py:382
  68.0 113.3 %conditional.9 = (bf16[64,2560]{1,0:T(8,128)(2,1)}, bf16[64,2560]{1,0:T(8,128)(2,1)S(1)}, f32[512,768]{1,0:T(8,128)}, f32[512,768]{1,0:T(8,128)}, f32[512,768]{1,0:T(8,128)}, /*index=5*/f32[512,768]{1,0:T(8,128)}) conditional(s32[]{:T(128)} %convert_element_type.164, (s32[]{:T(128)}, bf16[512,2560]{1,0:T(8,128)(2,1)S(1)}, ...), branch_computations={%region_8.11_spmd, %region_11.13_spmd} | conditional | flops 2013265920 | bytes 37166252 | solution.py:542
  68.1 10.1 %expert_forward.3 = (bf16[512,2560]{1,0:T(8,128)(2,1)}, f32[512,768]{1,0:T(8,128)}, f32[512,768]{1,0:T(8,128)}) custom-call(s32[1]{0:T(128)} %bitcast.pick_ref, bf16[512,2560]{1,0:T(8,128)(2,1)S(1)} %get-tuple-element.173.rows_hbm, bf16[2560,768]{1,0:T(8,128)(2,1)} %get-tuple-element.174.gate_a, bf16[2560,768]{1,0:T(8,128)(2,1)} %get-tuple-element.175.up_a, ...), custom_call_target="tpu_custom_call" | custom-call | tf_op jit(solution)/shard_map/cond/branch_1_fun/expert_forward/pallas_call | solution.py:196
  78.2 5.3 all-to-all-start
  83.6 21.9 %all-to-all-done = bf16[32,16,2560]{2,1,0:T(8,128)(2,1)S(1)} async-done(((bf16[32,16,2560]{2,1,0:T(8,128)(2,1)}), bf16[32,16,2560]{2,1,0:T(8,128)(2,1)S(1)}, u32[]{:S(2)}, u32[]{:S(2)}) %all-to-all-start) | async-done | bytes 2621472 | tf_op jit(solution)/shard_map/cond/branch_1_fun/all_to_all | solution.py:382
  106.1 0.9 fusion.9
  107.0 1.9 convolution_convert_fusion
  108.9 32.2 %all_to_all.61 = bf16[32,16,2560]{2,1,0:T(8,128)(2,1)} all-to-all(bf16[32,16,2560]{2,1,0:T(8,128)(2,1)S(1)} %bitcast.177), channel_id=1, replica_groups=mesh['segment'=4,'expert'=32] {'expert'}, dimensions={0} | all-to-all | bytes 5242880 | tf_op jit(solution)/shard_map/cond/branch_1_fun/all_to_all | solution.py:382
  141.1 10.2 %expert_forward.4 = (bf16[512,2560]{1,0:T(8,128)(2,1)}, f32[512,768]{1,0:T(8,128)}, f32[512,768]{1,0:T(8,128)}) custom-call(s32[1]{0:T(128)} %bitcast.3.pick_ref, bf16[512,2560]{1,0:T(8,128)(2,1)} %bitcast.185, bf16[2560,768]{1,0:T(8,128)(2,1)} %get-tuple-element.174.gate_a, bf16[2560,768]{1,0:T(8,128)(2,1)} %get-tuple-element.175.up_a, ...), custom_call_target="tpu_custom_call" | custom-call | tf_op jit(solution)/shard_map/cond/branch_1_fun/expert_forward/pallas_call | solution.py:196
  151.3 4.1 all-to-all-start.2
  155.4 23.9 %all-to-all-done.2 = bf16[32,16,2560]{2,1,0:T(8,128)(2,1)S(1)} async-done(((bf16[32,16,2560]{2,1,0:T(8,128)(2,1)}), bf16[32,16,2560]{2,1,0:T(8,128)(2,1)S(1)}, u32[]{:S(2)}, u32[]{:S(2)}) %all-to-all-start.2) | async-done | bytes 2621472 | tf_op jit(solution)/shard_map/cond/branch_1_fun/all_to_all | solution.py:382
  179.9 1.1 fusion.12
  181.4 1.3 collective-permute-start.6
  182.7 4.0 collective-permute-done.6.anchor_ref
  186.7 15.7 %conditional.10 = (bf16[64,2560]{1,0:T(8,128)(2,1)S(1)}, bf16[512,768]{1,0:T(8,128)(2,1)}, bf16[64,2560]{1,0:T(8,128)(2,1)}, bf16[64,2560]{1,0:T(8,128)(2,1)}) conditional(s32[]{:T(128)} %convert_element_type.164, (bf16[64,2560]{1,0:T(8,128)(2,1)S(1)}, f32[64,512]{1,0:T(8,128)}, s32[]{:T(128)}, f32[1,2560]{1,0:T(1,128)S(1)}, ...), branch_computations={%region_14.19_spmd, %region_19.20_spmd} | conditional | flops 1186922752 | bytes 65049364 | solution.py:565
  199.9 0.9 broadcast.209
  202.3 1.3 collective-permute-start.7
  204.2 212.1 %collective-permute-done.7.anchor_ref = bf16[64,2560]{1,0:T(8,128)(2,1)S(1)} collective-permute-done((bf16[64,2560]{1,0:T(8,128)(2,1)}, bf16[64,2560]{1,0:T(8,128)(2,1)S(1)}, u32[]{:S(2)}, u32[]{:S(2)}) %collective-permute-start.7) | collective-permute-done | bytes 327712 | tf_op jit(solution)/shard_map/ppermute | solution.py:568
  416.2 2.1 held_back.5
  418.3 137.9 %conditional.11 = (bf16[64,2560]{1,0:T(8,128)(2,1)S(1)}, bf16[64,2560]{1,0:T(8,128)(2,1)}, bf16[64,2560]{1,0:T(8,128)(2,1)}, bf16[1,64,2560]{2,1,0:T(8,128)(2,1)}) conditional(s32[]{:T(128)} %convert_element_type.164, (bf16[64,2560]{1,0:T(8,128)(2,1)S(1)}, f32[64,512]{1,0:T(8,128)S(1)}, s32[]{:T(128)}, bf16[512,768]{1,0:T(8,128)(2,1)}, ...), branch_computations={%region_20.23_spmd, %region_23.29_spmd} | conditional | flops 2349858816 | bytes 45726884 | solution.py:587
  418.4 1.7 multiply_convert_fusion.2
  420.1 25.5 %all_to_all.66 = bf16[32,16,2560]{2,1,0:T(8,128)(2,1)} all-to-all(bf16[32,16,2560]{2,1,0:T(8,128)(2,1)S(1)} %bitcast.179), channel_id=1, replica_groups=mesh['segment'=4,'expert'=32] {'expert'}, dimensions={0} | all-to-all | bytes 5242880 | tf_op jit(solution)/shard_map/cond/branch_1_fun/all_to_all | solution.py:382
  445.5 12.1 %expert_backward.4 = bf16[512,2560]{1,0:T(8,128)(2,1)} custom-call(s32[1]{0:T(128)} %bitcast.32.pick_ref, bf16[512,2560]{1,0:T(8,128)(2,1)} %bitcast.167, f32[512,768]{1,0:T(8,128)} %get-tuple-element.231.pre_hbm, f32[512,768]{1,0:T(8,128)} %get-tuple-element.232.val_hbm, bf16[2560,768]{1,0:T(8,128)(2,1)} %get-tuple-element.233.gate_a, ...), custom_call_target="tpu_custom_call" | custom-call | tf_op jit(solution)/shard_map/cond/branch_1_fun/expert_backward/pallas_call | solution.py:282
  457.6 4.1 all-to-all-start.11
  461.8 21.2 %all-to-all-done.11 = bf16[32,16,2560]{2,1,0:T(8,128)(2,1)S(1)} async-done(((bf16[32,16,2560]{2,1,0:T(8,128)(2,1)}), bf16[32,16,2560]{2,1,0:T(8,128)(2,1)S(1)}, u32[]{:S(2)}, u32[]{:S(2)}) %all-to-all-start.11) | async-done | bytes 2621472 | tf_op jit(solution)/shard_map/cond/branch_1_fun/all_to_all | solution.py:382
  483.0 1.6 fusion.61
  484.7 2.0 fusion.64
  486.7 1.9 multiply_convert_fusion.1
  488.5 26.8 %all_to_all.67 = bf16[32,16,2560]{2,1,0:T(8,128)(2,1)} all-to-all(bf16[32,16,2560]{2,1,0:T(8,128)(2,1)S(1)} %bitcast.182), channel_id=1, replica_groups=mesh['segment'=4,'expert'=32] {'expert'}, dimensions={0} | all-to-all | bytes 5242880 | tf_op jit(solution)/shard_map/cond/branch_1_fun/all_to_all | solution.py:382
  515.3 12.1 %expert_backward.5 = bf16[512,2560]{1,0:T(8,128)(2,1)} custom-call(s32[1]{0:T(128)} %bitcast.38.pick_ref, bf16[512,2560]{1,0:T(8,128)(2,1)} %bitcast.168, f32[512,768]{1,0:T(8,128)} %get-tuple-element.245.pre_hbm, f32[512,768]{1,0:T(8,128)} %get-tuple-element.246.val_hbm, bf16[2560,768]{1,0:T(8,128)(2,1)} %get-tuple-element.233.gate_a, ...), custom_call_target="tpu_custom_call" | custom-call | tf_op jit(solution)/shard_map/cond/branch_1_fun/expert_backward/pallas_call | solution.py:282
  527.5 4.2 all-to-all-start.13
  531.7 1.0 copy.101
  532.7 1.7 copy.104
  534.4 19.2 %all-to-all-done.13 = bf16[32,16,2560]{2,1,0:T(8,128)(2,1)S(1)} async-done(((bf16[32,16,2560]{2,1,0:T(8,128)(2,1)}), bf16[32,16,2560]{2,1,0:T(8,128)(2,1)S(1)}, u32[]{:S(2)}, u32[]{:S(2)}) %all-to-all-start.13) | async-done | bytes 2621472 | tf_op jit(solution)/shard_map/cond/branch_1_fun/all_to_all | solution.py:382
  554.3 2.0 fusion.69
  556.3 1.3 broadcast_select_fusion.3
  557.7 2.0 collective-permute-done.8
  559.8 1.2 broadcast_select_fusion
  (71 shorter events, 7.8 us)
Async XLA Ops:
  0.6 7.1 %collective-permute-start.2 = (f32[1,2560]{1,0:T(1,128)}, f32[1,2560]{1,0:T(1,128)S(1)}, u32[]{:S(2)}, u32[]{:S(2)}) collective-permute-start(f32[1,2560]{1,0:T(1,128)} %param.20), channel_id=1, source_target_pairs={{0,32},{32,0},{64,96},{96,64},{1,33},{33,1},{65,97},{97,65},{2,34}... | collective-permute-start | bytes 30728 | tf_op jit(solution)/shard_map/ppermute | solution.py:459
  2.9 3.1 collective-permute-start
  3.8 3.1 collective-permute-start.1
  4.3 63.7 %collective-permute-start.3 = (bf16[768,2560]{1,0:T(8,128)(2,1)}, bf16[768,2560]{1,0:T(8,128)(2,1)}, u32[]{:S(2)}, u32[]{:S(2)}) collective-permute-start(bf16[768,2560]{1,0:T(8,128)(2,1)} %bitcast.156), channel_id=1, source_target_pairs={{0,32},{32,0},{64,96},{96,64},{1,33},{33,1},{65,97},{97,65},{2,34}... | collective-permute-start | bytes 11796488 | tf_op jit(solution)/shard_map/ppermute | solution.py:459
  4.4 63.6 %collective-permute-start.4 = (bf16[2560,768]{1,0:T(8,128)(2,1)}, bf16[2560,768]{1,0:T(8,128)(2,1)}, u32[]{:S(2)}, u32[]{:S(2)}) collective-permute-start(bf16[2560,768]{1,0:T(8,128)(2,1)} %bitcast.148), channel_id=1, source_target_pairs={{0,32},{32,0},{64,96},{96,64},{1,33},{33,1},{65,97},{97,65},{2,34}... | collective-permute-start | bytes 11796488 | tf_op jit(solution)/shard_map/ppermute | solution.py:459
  6.0 62.1 %copy-start = (bf16[64,2560]{1,0:T(8,128)(2,1)}, bf16[64,2560]{1,0:T(8,128)(2,1)S(1)}, u32[]{:S(2)}) copy-start(bf16[64,2560]{1,0:T(8,128)(2,1)S(1)} %get-tuple-element.302) | copy-start | bytes 983044
  6.0 62.0 %collective-permute-start.5 = (bf16[2560,768]{1,0:T(8,128)(2,1)}, bf16[2560,768]{1,0:T(8,128)(2,1)}, u32[]{:S(2)}, u32[]{:S(2)}) collective-permute-start(bf16[2560,768]{1,0:T(8,128)(2,1)} %bitcast.152), channel_id=1, source_target_pairs={{0,32},{32,0},{64,96},{96,64},{1,33},{33,1},{65,97},{97,65},{2,34}... | collective-permute-start | bytes 11796488 | tf_op jit(solution)/shard_map/ppermute | solution.py:459
  35.9 11.7 %copy-start.7 = (bf16[64,512]{1,0:T(8,128)(2,1)S(1)}, bf16[64,512]{1,0:T(8,128)(2,1)}, u32[]{:S(2)}) copy-start(bf16[64,512]{1,0:T(8,128)(2,1)} %get-tuple-element.292.value_ref) | copy-start | bytes 196612
  35.9 32.1 %all-to-all-start.14 = ((bf16[32,16,2560]{2,1,0:T(8,128)(2,1)}), bf16[32,16,2560]{2,1,0:T(8,128)(2,1)S(1)}, u32[]{:S(2)}, u32[]{:S(2)}) async-start(bf16[32,16,2560]{2,1,0:T(8,128)(2,1)} %bitcast.54), calls=%async_computation.14 | async-start | bytes 5242880 | tf_op jit(solution)/shard_map/all_to_all | solution.py:382
  78.2 5.3 copy-start.8
  78.2 5.3 copy-start.5
  78.2 27.3 %all-to-all-start = ((bf16[32,16,2560]{2,1,0:T(8,128)(2,1)}), bf16[32,16,2560]{2,1,0:T(8,128)(2,1)S(1)}, u32[]{:S(2)}, u32[]{:S(2)}) async-start(bf16[32,16,2560]{2,1,0:T(8,128)(2,1)} %bitcast.188), calls=%async_computation | async-start | bytes 5242880 | tf_op jit(solution)/shard_map/cond/branch_1_fun/all_to_all | solution.py:382
  151.3 28.0 %all-to-all-start.2 = ((bf16[32,16,2560]{2,1,0:T(8,128)(2,1)}), bf16[32,16,2560]{2,1,0:T(8,128)(2,1)S(1)}, u32[]{:S(2)}, u32[]{:S(2)}) async-start(bf16[32,16,2560]{2,1,0:T(8,128)(2,1)} %bitcast.190), calls=%async_computation.2 | async-start | bytes 5242880 | tf_op jit(solution)/shard_map/cond/branch_1_fun/all_to_all | solution.py:382
  181.4 5.3 copy-start.3
  181.4 5.3 collective-permute-start.6
  202.3 213.9 %collective-permute-start.7 = (bf16[64,2560]{1,0:T(8,128)(2,1)}, bf16[64,2560]{1,0:T(8,128)(2,1)S(1)}, u32[]{:S(2)}, u32[]{:S(2)}) collective-permute-start(bf16[64,2560]{1,0:T(8,128)(2,1)} %get-tuple-element.274), channel_id=1, source_target_pairs={{64,0},{96,32},{65,1},{97,33},{66,2},{98,34},{67,3},{99,35},{68,4}... | collective-permute-start | bytes 983048 | tf_op jit(solution)/shard_map/ppermute | solution.py:568
  457.6 4.1 copy-start.10
  457.6 25.4 %all-to-all-start.11 = ((bf16[32,16,2560]{2,1,0:T(8,128)(2,1)}), bf16[32,16,2560]{2,1,0:T(8,128)(2,1)S(1)}, u32[]{:S(2)}, u32[]{:S(2)}) async-start(bf16[32,16,2560]{2,1,0:T(8,128)(2,1)} %bitcast.165), calls=%async_computation.11 | async-start | bytes 5242880 | tf_op jit(solution)/shard_map/cond/branch_1_fun/all_to_all | solution.py:382
  527.5 26.2 %copy-start.1 = (bf16[64,2560]{1,0:T(8,128)(2,1)S(1)}, bf16[64,2560]{1,0:T(8,128)(2,1)}, u32[]{:S(2)}) copy-start(bf16[64,2560]{1,0:T(8,128)(2,1)} %get-tuple-element.240) | copy-start | bytes 983044 | tf_op jit(solution)/shard_map/cond
  527.5 26.1 %all-to-all-start.13 = ((bf16[32,16,2560]{2,1,0:T(8,128)(2,1)}), bf16[32,16,2560]{2,1,0:T(8,128)(2,1)S(1)}, u32[]{:S(2)}, u32[]{:S(2)}) async-start(bf16[32,16,2560]{2,1,0:T(8,128)(2,1)} %bitcast.163), calls=%async_computation.13 | async-start | bytes 5242880 | tf_op jit(solution)/shard_map/cond/branch_1_fun/all_to_all | solution.py:382
  556.3 3.5 copy-start.14
  557.6 2.2 collective-permute-start.8
